TPU v7x, 32 devices: a whole 2x2x4 slice. The times are simulated.
32 devices in a mesh: dp: 8 (over z, y), var: 4 (over x, core).
Axes of the slice: x: 2, y: 2, z: 4, core: 2. Of those that a mesh axis runs over, the one named last changes fastest.
Arguments:
- img_lo: bfloat16 [320, 128, 320], P('dp', None, 'var'), may hold values from -6 to 6
- img_hi: bfloat16 [160, 512, 320], P('dp', None, 'var'), may hold values from -6 to 6
- keep_lo: int32 [320, 32], P('dp'), may hold values from 0 to 127, as said below
- keep_hi: int32 [160, 128], P('dp'), may hold values from 0 to 511, as said below
- mask_lo: int32 [320, 32], P('dp'), may hold values 0 or 1
- mask_hi: int32 [160, 128], P('dp'), may hold values 0 or 1
- w_embed: bfloat16 [320, 768], P('var'), may hold values from -0.3125 to 0.3125
- pos_lo: bfloat16 [128, 768], replicated, may hold values from -3 to 3
- pos_hi: bfloat16 [512, 768], replicated, may hold values from -3 to 3
- ln1_gain: float32 [768], replicated, may hold values from 0.25 to 1.75
- w_qkv: bfloat16 [768, 2304], replicated, may hold values from -0.21875 to 0.21875
- w_out: bfloat16 [768, 768], replicated, may hold values from -0.625 to 0.625
- ln2_gain: float32 [768], replicated, may hold values from 0.25 to 1.75
- w_fc1: bfloat16 [768, 3072], replicated, may hold values from -0.21875 to 0.21875
- b_fc1: float32 [3072], replicated, may hold values from -3 to 3
- w_fc2: bfloat16 [3072, 768], replicated, may hold values from -0.109375 to 0.109375
- b_fc2: float32 [768], replicated, may hold values from -3 to 3
- w_head: bfloat16 [768, 320], P(None, 'var'), may hold values from -0.21875 to 0.21875
- cot_lo: bfloat16 [320, 32, 320], P('dp', None, 'var'), may hold values from -6 to 6
- cot_hi: bfloat16 [160, 128, 320], P('dp', None, 'var'), may hold values from -6 to 6
Outputs:
- pred_lo: bfloat16 [320, 32, 320], P('dp', None, 'var')
- pred_hi: bfloat16 [160, 128, 320], P('dp', None, 'var')
- grad_img_lo: bfloat16 [320, 128, 320], P('dp', None, 'var')
- grad_img_hi: bfloat16 [160, 512, 320], P('dp', None, 'var')
- grad_embed: float32 [320, 768], P('var')
- grad_pos_lo: float32 [128, 768], P(('dp', 'var'))
- grad_pos_hi: float32 [512, 768], P(('dp', 'var'))
- grad_ln1: float32 [768], P(('dp', 'var'))
- grad_qkv: float32 [768, 2304], P(('dp', 'var'))
- grad_out: float32 [768, 768], P(('dp', 'var'))
- grad_ln2: float32 [768], P(('dp', 'var'))
- grad_fc1: float32 [768, 3072], P(('dp', 'var'))
- grad_b1: float32 [3072], P(('dp', 'var'))
- grad_fc2: float32 [3072, 768], P(('dp', 'var'))
- grad_b2: float32 [768], P(('dp', 'var'))
- grad_head: float32 [768, 320], P(None, 'var')
Inputs may be any that keep to these rules, and one draw needn't show every extreme that they name: `keep_lo`: each row names 32 different patches of its sample. `keep_hi`: each row names 128 different patches of its sample. `mask_lo`: slot 0 counts as visible whatever its entry. `mask_hi`: slot 0 counts as visible whatever its entry.
All inputs are finite; a program needn't handle non-finite values. No bound on the sum of `mask_lo` or of `mask_hi` on one device may be relied on, other than what follows from the above.
Results may differ from a plain program's by a relative error of at most 0.02.
Values may be sent and summed in bfloat16 or wider, within the bound.
No kernel may reach another device: no remote copies, remote signals or barrier semaphores. Data moves between devices by JAX's collectives and lax.ppermute only.
A program may use at most 256 MiB of HBM per device.

v0:
```python
import functools
import math

import jax
import jax.numpy as jnp
from jax import lax
from jax.experimental import pallas as pl
from jax.experimental.pallas import tpu as pltpu
from jax.sharding import PartitionSpec as P

HEADS = 12
EPSILON = 1e-06
AXES = ("dp", "var")
BF16 = jnp.bfloat16
F32 = jnp.float32
LANES = 128
ROWS = 256
MASKED = -1000000000.0
SHARE = 0.5


def dot(left, right, dims):
    return lax.dot_general(left, right, (dims, ((), ())), preferred_element_type=F32)


def nn(left, right):
    return dot(left, right, ((1,), (0,)))


def nt(left, right):
    return dot(left, right, ((1,), (1,)))


def tn(left, right):
    return dot(left, right, ((0,), (0,)))


def shape(dims, dtype):
    return jax.ShapeDtypeStruct(dims, dtype)


def whole(array):
    zeros = (0,) * array.ndim
    return pl.BlockSpec(array.shape, lambda *_: zeros, pipeline_mode=pl.Buffered(1))


def across(rows, width):
    return pl.BlockSpec((rows, width), lambda i, *_: (i, 0))


def along(height, columns):
    return pl.BlockSpec((height, columns), lambda i, *_: (0, i))


def fixed(*dims):
    zeros = (0,) * len(dims)
    return pl.BlockSpec(dims, lambda *_: zeros)


def params(mebibytes):
    return pltpu.CompilerParams(vmem_limit_bytes=mebibytes << 20)


def cost(flops, nbytes):
    return pl.CostEstimate(flops=int(flops * SHARE), bytes_accessed=int(nbytes * SHARE), transcendentals=0)


def iota(dims, axis):
    return lax.broadcasted_iota(jnp.int32, dims, axis)


def accumulate(ref, first, value):
    @pl.when(first)
    def _():
        ref[...] = value

    @pl.when(jnp.logical_not(first))
    def _():
        ref[...] += value


def normalize(values):
    center = values - jnp.mean(values, axis=-1, keepdims=True)
    inverse = lax.rsqrt(jnp.mean(center * center, axis=-1, keepdims=True) + EPSILON)
    return center * inverse, inverse


def normalize_back(upstream, normed, inverse, gains):
    scaled = upstream * gains
    mean_plain = jnp.mean(scaled, axis=-1, keepdims=True)
    mean_mixed = jnp.mean(scaled * normed, axis=-1, keepdims=True)
    return inverse * (scaled - mean_plain - normed * mean_mixed)


def gelu_parts(u):
    ratio = 1.0 / (1.0 + (0.3275911 * math.sqrt(0.5)) * jnp.abs(u))
    bell = jnp.exp(-0.5 * u * u)
    series = 0.5 * 1.061405429
    for factor in (-1.453152027, 1.421413741, -0.284496736, 0.254829592):
        series = series * ratio + 0.5 * factor
    tail = series * ratio * bell
    below = jnp.where(u < 0, tail, 1.0 - tail)
    return u * below, below + u * (bell * (1.0 / math.sqrt(2.0 * math.pi)))


class Sizes:
    def __init__(self, keep_lo, keep_hi, w_embed, img_lo, img_hi, groups):
        self.lo_each, self.hi_each = keep_lo[0] // groups, keep_hi[0] // groups
        self.lo_length, self.hi_length = keep_lo[1], keep_hi[1]
        self.features, self.width = w_embed
        self.lo_patches, self.hi_patches = img_lo[1], img_hi[1]
        self.groups = groups
        self.pack = LANES // self.lo_length
        self.lo_tiles = -(-self.lo_each // self.pack)
        self.hi_rows = self.hi_each * self.hi_length
        tiles = self.hi_each + self.lo_tiles
        self.tiles = tiles + tiles % 2
        self.rows = self.tiles * LANES


def sample_tiles(s):
    out = []
    for t in range(s.tiles - s.hi_each):
        first = t * s.pack
        out.append((s.hi_each + t, first, max(0, min(s.pack, s.lo_each - first))))
    return out


def slots(rows, fill, s):
    missing = s.pack - len(rows)
    if missing:
        rows = rows + [jnp.full((1, missing * s.lo_length), fill, rows[0].dtype if rows else jnp.int32)]
    return rows[0] if len(rows) == 1 else jnp.concatenate(rows, axis=1)


def pick_kernel(s, members, member_ref, keep_lo_ref, keep_hi_ref, img_lo_ref, img_hi_ref, *out_refs):
    for k, out_ref in zip(members, out_refs):
        other = member_ref[0] ^ k
        for i in range(s.hi_each):
            at = other * s.hi_each + i
            chosen = iota((s.hi_patches, LANES), 0) == keep_hi_ref[pl.ds(at, 1), :]
            got = nn(img_hi_ref[at], jnp.where(chosen, 1.0, 0.0).astype(BF16))
            out_ref[:, i * LANES : (i + 1) * LANES] = got.astype(BF16)
        for tile, first, count in sample_tiles(s):
            parts = []
            for j in range(count):
                at = other * s.lo_each + first + j
                chosen = iota((s.lo_patches, s.lo_length), 0) == keep_lo_ref[pl.ds(at, 1), :]
                parts.append(nn(img_lo_ref[at], jnp.where(chosen, 1.0, 0.0).astype(BF16)))
            if count < s.pack:
                parts.append(jnp.zeros((s.features, (s.pack - count) * s.lo_length), F32))
            joined = jnp.concatenate(parts, axis=1) if len(parts) > 1 else parts[0]
            out_ref[:, tile * LANES : (tile + 1) * LANES] = joined.astype(BF16)


def pick(s, members, member, keep_lo, keep_hi, img_lo, img_hi):
    args = (keep_lo, keep_hi, img_lo, img_hi)
    return pl.pallas_call(
        functools.partial(pick_kernel, s, members),
        grid_spec=pltpu.PrefetchScalarGridSpec(
            num_scalar_prefetch=1,
            grid=(1,),
            in_specs=[whole(a) for a in args],
            out_specs=[fixed(s.features, s.rows)] * len(members),
        ),
        out_shape=[shape((s.features, s.rows), BF16)] * len(members),
        compiler_params=params(60),
        cost_estimate=cost(2e9, 4e6),
    )(member, *args)


def stage_kernel(s, member_ref, keep_lo_ref, keep_hi_ref, mask_lo_ref, mask_hi_ref, cot_lo_ref, cot_hi_ref, keep_ref, seen_ref, *out_refs):
    eye = jnp.where(iota((s.features, s.features), 0) == iota((s.features, s.features), 1), 1.0, 0.0).astype(BF16)
    first_hi = (iota((1, s.hi_length), 1) == 0).astype(jnp.int32)
    first_lo = (iota((1, s.lo_length), 1) == 0).astype(jnp.int32)
    for k, out_ref in enumerate(out_refs):
        other = member_ref[0] ^ k
        for i in range(s.hi_each):
            at = other * s.hi_each + i
            keep_ref[k, i : i + 1, :] = keep_hi_ref[pl.ds(at, 1), :]
            out_ref[:, i * LANES : (i + 1) * LANES] = cot_hi_ref[at]
            if k == 0:
                seen_ref[i : i + 1, :] = jnp.maximum(mask_hi_ref[pl.ds(at, 1), :], first_hi).astype(F32)
        for tile, first, count in sample_tiles(s):
            begin = other * s.lo_each + first
            keep_ref[k, tile : tile + 1, :] = slots([keep_lo_ref[pl.ds(begin + j, 1), :] for j in range(count)], -1, s)
            if k == 0:
                seen = [jnp.maximum(mask_lo_ref[pl.ds(begin + j, 1), :], first_lo) for j in range(count)]
                seen_ref[tile : tile + 1, :] = slots(seen, 0, s).astype(F32)
            where = slice(tile * LANES, (tile + 1) * LANES)
            if count < s.pack:
                out_ref[:, where] = jnp.zeros((s.features, LANES), BF16)
            if count:
                size = count * s.lo_length
                start = pl.multiple_of(begin * s.lo_length, s.lo_length)
                out_ref[:, tile * LANES : tile * LANES + size] = nt(eye, cot_lo_ref[pl.ds(start, size), :]).astype(BF16)


def stage(s, member, keep_lo, keep_hi, mask_lo, mask_hi, cot_lo, cot_hi):
    args = (keep_lo, keep_hi, mask_lo, mask_hi, cot_lo, cot_hi)
    return pl.pallas_call(
        functools.partial(stage_kernel, s),
        grid_spec=pltpu.PrefetchScalarGridSpec(
            num_scalar_prefetch=1,
            grid=(1,),
            in_specs=[whole(a) for a in args],
            out_specs=[fixed(s.groups, s.tiles, LANES), fixed(s.tiles, LANES)]
            + [fixed(s.features, s.rows)] * s.groups,
        ),
        out_shape=[shape((s.groups, s.tiles, LANES), jnp.int32), shape((s.tiles, LANES), F32)]
        + [shape((s.features, s.rows), BF16)] * s.groups,
        compiler_params=params(60),
        cost_estimate=cost(1e8, 4e6),
    )(member, *args)


def chosen_columns(s, keep_ref, tile, patches, wanted_hi):
    row = keep_ref[pl.ds(tile, 1), :]
    is_hi = tile < s.hi_each
    row = jnp.where(is_hi if wanted_hi else jnp.logical_not(is_hi), row, -1)
    column = jnp.broadcast_to(row.astype(F32), (LANES, LANES)).T.astype(jnp.int32)
    parts = [jnp.where(iota((LANES, LANES), 1) + at == column, 1.0, 0.0) for at in range(0, patches, LANES)]
    return jnp.concatenate(parts, axis=1).astype(BF16)


def pair_masks():
    lane = iota((1, LANES), 1)
    low = jnp.where(lane < LANES // 2, 1.0, 0.0).astype(BF16)
    high = jnp.where(lane < LANES // 2, 0.0, 1.0).astype(BF16)
    return low, high


def doubled(block, masks):
    return jnp.concatenate([block * masks[0], block * masks[1]], axis=0)


def allowed(s, seen_ref, tile):
    bits = jnp.where(tile < s.hi_each, s.hi_length.bit_length() - 1, s.lo_length.bit_length() - 1)
    same = (iota((LANES, LANES), 0) >> bits) == (iota((LANES, LANES), 1) >> bits)
    open_to = jnp.logical_and(same, seen_ref[pl.ds(tile, 1), :] > 0)
    return jnp.concatenate([open_to, open_to], axis=0)


def forward_kernel(s, heads, keep_ref, seen_ref, p0, p1, p2, p3, w0, w1, w2, w3, pos_lo_ref, pos_hi_ref, gain1_ref, wqkv_ref, wout_ref, x0_ref, a_ref, qkv_ref, probs_ref, mixed_ref, x1_ref):
    step = pl.program_id(0)
    per = ROWS // LANES
    width = s.width
    picked = jnp.concatenate([p[...] for p in (p0, p1, p2, p3)], axis=0)
    embed = jnp.concatenate([w[: s.features, :] for w in (w0, w1, w2, w3)], axis=0)
    hot_hi = jnp.concatenate([chosen_columns(s, keep_ref, step * per + j, s.hi_patches, True) for j in range(per)], axis=0)
    hot_lo = jnp.concatenate([chosen_columns(s, keep_ref, step * per + j, s.lo_patches, False) for j in range(per)], axis=0)
    start = tn(picked, embed) + (nn(hot_hi, pos_hi_ref[...]) + nn(hot_lo, pos_lo_ref[...]))
    x0_ref[...] = start.astype(BF16)
    normed, _ = normalize(start)
    normed = (normed * gain1_ref[...]).astype(BF16)
    a_ref[...] = normed
    for c in range(3):
        part = slice(c * width, (c + 1) * width)
        qkv_ref[:, part] = nn(normed, wqkv_ref[:, part]).astype(BF16)
    masks = pair_masks()
    scale = 1.0 / math.sqrt(width // heads)
    for j in range(per):
        rows = slice(j * LANES, (j + 1) * LANES)
        ok = allowed(s, seen_ref, step * per + j)
        for h in range(width // LANES):
            at = h * LANES
            q = qkv_ref[rows, at : at + LANES]
            k = qkv_ref[rows, width + at : width + at + LANES]
            v = qkv_ref[rows, 2 * width + at : 2 * width + at + LANES]
            scores = nt(doubled(q, masks), k) * scale
            scores = jnp.where(ok, scores, MASKED)
            raised = jnp.exp(scores - jnp.max(scores, axis=-1, keepdims=True))
            probs = raised / jnp.sum(raised, axis=-1, keepdims=True)
            rounded = probs.astype(BF16)
            probs_ref[j, h] = rounded
            wide = jnp.concatenate([rounded[:LANES], rounded[LANES:]], axis=1)
            mixed_ref[rows, at : at + LANES] = nn(wide, doubled(v, masks)).astype(BF16)
    middle = start + nn(mixed_ref[...], wout_ref[...])
    x1_ref[...] = middle


def forward(s, heads, keep, seen, picked, weights, pos_lo, pos_hi, gain1, wqkv, wout):
    width, rows = s.width, s.rows
    per, pairs = ROWS // LANES, width // LANES
    return pl.pallas_call(
        functools.partial(forward_kernel, s, heads),
        grid=(rows // ROWS,),
        in_specs=[whole(keep), whole(seen)]
        + [along(s.features, ROWS)] * 4
        + [whole(w) for w in weights]
        + [whole(a) for a in (pos_lo, pos_hi, gain1, wqkv, wout)],
        out_specs=[
            across(ROWS, width),
            across(ROWS, width),
            across(ROWS, 3 * width),
            pl.BlockSpec((per, pairs, 2 * LANES, LANES), lambda i: (i, 0, 0, 0)),
            across(ROWS, width),
            across(ROWS, width),
        ],
        out_shape=[
            shape((rows, width), BF16),
            shape((rows, width), BF16),
            shape((rows, 3 * width), BF16),
            shape((s.tiles, pairs, 2 * LANES, LANES), BF16),
            shape((rows, width), BF16),
            shape((rows, width), F32),
        ],
        compiler_params=params(60),
        cost_estimate=cost(1.5e10, 3e7),
    )(keep, seen, *picked, *weights, pos_lo, pos_hi, gain1, wqkv, wout)


def part_rows(width, offset):
    return pl.BlockSpec((ROWS, width), lambda i, *_: (i + offset, 0))


def relative(ids_ref, x, y, z, c):
    return ids_ref[0] ^ (2 * z + y), ids_ref[1] ^ (2 * x + c)


def places(ids_ref, far):
    out = []
    for c in range(2):
        for x in range(2):
            for y in range(2):
                for z in range(far):
                    d, v = relative(ids_ref, x, y, z, c)
                    out.append(d * 4 + v)
    return out


def turn_relative(ids_ref, far, block, source_ref, turned_ref, acc_ref):
    order = places(ids_ref, far)
    rows = source_ref.shape[0]
    for begin in range(0, rows, rows // 2):
        span = slice(begin, begin + rows // 2)
        acc_ref[:, : rows // 2] = source_ref[span, :].astype(F32).T
        for p in range(0, len(order), 2):
            pair = [
                acc_ref[pl.ds(pl.multiple_of(at * block, 8), block), : rows // 2]
                for at in order[p : p + 2]
            ]
            turned_ref[p * block : (p + 2) * block, span] = jnp.concatenate(pair, axis=0).astype(BF16)


def spread(ids_ref, far, acc_ref, outs, block, extra):
    for x in range(2):
        for y in range(2):
            for z in range(far):
                for c, out_ref in enumerate(outs):
                    d, v = relative(ids_ref, x, y, z, c)
                    start = pl.multiple_of((d * 4 + v) * block, 8)
                    out_ref[x, y, z, :block, :] = acc_ref[pl.ds(start, block), :].astype(BF16)
                    out_ref[x, y, z, block:, :] = extra


def spread_features(s, ids_ref, acc_ref, outs):
    half = s.features // 2
    for k in range(4):
        for y in range(2):
            start = k * s.features + ((ids_ref[0] & 1) ^ y) * half
            rows = acc_ref[pl.ds(pl.multiple_of(start, 8), half), :]
            outs[k % 2][k // 2, y] = rows.astype(BF16)


def hidden_kernel(s, far, chunks, ids_ref, seen_ref, c0, c1, c2, c3, h0, h1, h2, h3, x1_ref, mixed_ref, w1_ref, b1_ref, w2_ref, b2_ref, gain2_ref, wout_ref, two0_ref, two1_ref, one0_ref, one1_ref, p0, p1, p2, p3, out0_ref, out1_ref, n0_ref, n1_ref, go_ref, ga_ref, b_ref, turned_ref, gm_ref, gpred_ref, forth_ref, back_ref, z_ref, gu_ref, acc_ref, side_ref):
    step = pl.program_id(0)
    width = s.width
    block = width // (8 * far)
    subs = [slice(begin, begin + ROWS) for begin in range(0, s.rows, ROWS)]
    seen = jnp.concatenate([seen_ref[t : t + 1, :] for t in range(s.tiles)], axis=1)

    @pl.when(step == 0)
    def _():
        gpred_ref[...] = jnp.concatenate([c[...] for c in (c0, c1, c2, c3)], axis=0) * seen.astype(BF16)
        head = jnp.concatenate([h[s.features :, :] for h in (h0, h1, h2, h3)], axis=0)
        total = None
        for rows in subs:
            values = x1_ref[rows, :]
            normed, _ = normalize(values)
            b_ref[rows, :] = (normed * gain2_ref[...]).astype(BF16)
            forth_ref[rows, :] = values + b2_ref[...]
            back_ref[rows, :] = jnp.zeros((ROWS, width), F32)
            upward = tn(gpred_ref[:, rows], head).astype(BF16)
            gm_ref[rows, :] = upward
            part = jnp.sum(upward.astype(F32), axis=0, keepdims=True)
            total = part if total is None else total + part
        side_ref[1:2, :] = total
        turn_relative(ids_ref, far, block, b_ref, turned_ref, acc_ref)

    @pl.when(step < chunks)
    def _():
        w1, w2, bias = w1_ref[...], w2_ref[...], b1_ref[...]
        total = None
        for rows in subs:
            u = nn(b_ref[rows, :], w1)
            upward = nt(gm_ref[rows, :], w2)
            z, slope = gelu_parts(u + bias)
            z = z.astype(BF16)
            gu = (upward * slope).astype(BF16)
            z_ref[rows, :] = z
            gu_ref[rows, :] = gu
            part = jnp.sum(gu.astype(F32), axis=0, keepdims=True)
            total = part if total is None else total + part
        side_ref[pl.ds(2 + ((ids_ref[0] >> 1) ^ step), 1), :] = total
        forth_ref[...] += nn(z_ref[...], w2)
        back_ref[...] += nt(gu_ref[...], w1)
        ones = nn(turned_ref[...], gu_ref[...])
        one0_ref[0] = ones[: width // 2].astype(BF16)
        one1_ref[0] = ones[width // 2 :].astype(BF16)
        acc_ref[...] = tn(z_ref[...], gm_ref[...])
        tall = width // 8
        for x in range(2):
            for y in range(2):
                for c, out_ref in enumerate((two0_ref, two1_ref)):
                    d, v = relative(ids_ref, x, y, 0, c)
                    start = pl.multiple_of(((d & 1) * 4 + v) * tall, 8)
                    out_ref[x, y, 0] = acc_ref[pl.ds(start, tall), :].astype(BF16)

    @pl.when(step == chunks)
    def _():
        total = None
        for rows in subs:
            z_ref[rows, :] = forth_ref[rows, :].astype(BF16)
            upward = back_ref[rows, :]
            normed, inverse = normalize(x1_ref[rows, :])
            part = jnp.sum(upward * normed, axis=0, keepdims=True)
            total = part if total is None else total + part
            grad = gm_ref[rows, :].astype(F32) + normalize_back(upward, normed, inverse, gain2_ref[...])
            grad = grad.astype(BF16)
            ga_ref[rows, :] = grad
            go_ref[rows, :] = nt(grad, wout_ref[...]).astype(BF16)
        side_ref[0:1, :] = total
        final = z_ref[...]
        for head, out in zip((h0, h1, h2, h3), (p0, p1, p2, p3)):
            out[...] = (nt(head[s.features :, :], final) * seen).astype(BF16)
        acc_ref[: s.groups * s.features, :] = nn(gpred_ref[...], final)
        spread_features(s, ids_ref, acc_ref, (n0_ref, n1_ref))
        acc_ref[...] = tn(mixed_ref[...], ga_ref[...])
        spread(ids_ref, far, acc_ref, (out0_ref, out1_ref), block, side_ref[...].astype(BF16))


def hidden(s, ids, far, seen, cots, weights, x1, mixed, w1, b1, w2, b2, gain2, wout):
    rows, width = s.rows, s.width
    chunks = w1.shape[1] // width
    block = width // (8 * far)
    high = s.groups * s.features
    sides = 8 * -(-(2 + chunks) // 8)
    last = chunks - 1

    def chunk(i, ids):
        return (ids[0] >> 1) ^ jnp.minimum(i, last)

    first = [seen, *cots, *weights, x1, mixed]
    rest = [b2, gain2, wout]
    outs = (
        [((2, 2, far, width // 8, width), BF16)] * 2
        + [((chunks, width // 2, width), BF16)] * 2
        + [((s.features, rows), BF16)] * 4
        + [((2, 2, far, block + sides, width), BF16)] * 2
        + [((2, 2, s.features // 2, width), BF16)] * 2
        + [((rows, width), BF16)] * 2
    )
    specs = [
        pl.BlockSpec((2, 2, 1, width // 8, width), lambda i, ids: (0, 0, jnp.minimum(i, last), 0, 0))
    ] * 2
    specs += [pl.BlockSpec((1, width // 2, width), lambda i, ids: (chunk(i, ids), 0, 0))] * 2
    specs += [fixed(*dims) for dims, _ in outs[4:]]
    return pl.pallas_call(
        functools.partial(hidden_kernel, s, far, chunks),
        grid_spec=pltpu.PrefetchScalarGridSpec(
            num_scalar_prefetch=1,
            grid=(chunks + 1,),
            in_specs=[whole(a) for a in first]
            + [
                pl.BlockSpec((width, width), lambda i, ids: (0, chunk(i, ids))),
                pl.BlockSpec((1, width), lambda i, ids: (0, chunk(i, ids))),
                pl.BlockSpec((width, width), lambda i, ids: (chunk(i, ids), 0)),
            ]
            + [whole(a) for a in rest],
            out_specs=specs,
            scratch_shapes=[
                pltpu.VMEM((rows, width), BF16),
                pltpu.VMEM((width, rows), BF16),
                pltpu.VMEM((rows, width), BF16),
                pltpu.VMEM((high, rows), BF16),
                pltpu.VMEM((rows, width), F32),
                pltpu.VMEM((rows, width), F32),
                pltpu.VMEM((rows, width), BF16),
                pltpu.VMEM((rows, width), BF16),
                pltpu.VMEM((width, width), F32),
                pltpu.VMEM((sides, width), F32),
            ],
        ),
        out_shape=[shape(*out) for out in outs],
        compiler_params=params(60),
        cost_estimate=cost(3.4e10, 4e7),
    )(ids, *first, w1, b1, w2, *rest)


def attention_back(s, heads, qkv_ref, probs_ref, go_ref, gqkv_ref):
    per = ROWS // LANES
    width = s.width
    masks = pair_masks()
    scale = 1.0 / math.sqrt(width // heads)
    for j in range(per):
        rows = slice(j * LANES, (j + 1) * LANES)
        for h in range(width // LANES):
            at = h * LANES
            q = doubled(qkv_ref[rows, at : at + LANES], masks)
            k = doubled(qkv_ref[rows, width + at : width + at + LANES], masks)
            v = qkv_ref[rows, 2 * width + at : 2 * width + at + LANES]
            out = doubled(go_ref[rows, at : at + LANES], masks)
            rounded = probs_ref[j, h]
            probs = rounded.astype(F32)
            upward = nt(out, v)
            centred = upward - jnp.sum(probs * upward, axis=-1, keepdims=True)
            grads = (probs * centred).astype(BF16)
            wide = jnp.concatenate([grads[:LANES], grads[LANES:]], axis=1)
            gqkv_ref[rows, at : at + LANES] = (nn(wide, k) * scale).astype(BF16)
            gqkv_ref[rows, width + at : width + at + LANES] = (tn(grads, q) * scale).astype(BF16)
            gqkv_ref[rows, 2 * width + at : 2 * width + at + LANES] = tn(rounded, out).astype(BF16)


def first_norm_back(gqkv, x0_ref, ga_ref, wqkv_ref, gain1_ref):
    upward = nt(gqkv, wqkv_ref[...])
    normed, inverse = normalize(x0_ref[...].astype(F32))
    grad = ga_ref[...].astype(F32) + normalize_back(upward, normed, inverse, gain1_ref[...])
    return grad.astype(BF16), jnp.sum(upward * normed, axis=0, keepdims=True)


def backward_kernel(s, heads, qkv_ref, probs_ref, go_ref, x0_ref, ga_ref, wqkv_ref, gain1_ref, gqkv_ref, g0_ref, gln1_ref):
    attention_back(s, heads, qkv_ref, probs_ref, go_ref, gqkv_ref)
    g0_ref[...], gain_part = first_norm_back(gqkv_ref[...], x0_ref, ga_ref, wqkv_ref, gain1_ref)
    accumulate(gln1_ref, pl.program_id(0) == 0, gain_part)


def row_inputs(s, offset):
    width = s.width
    return [
        part_rows(3 * width, offset),
        pl.BlockSpec((ROWS // LANES, width // LANES, 2 * LANES, LANES), lambda i, *_: (i + offset, 0, 0, 0)),
        part_rows(width, offset),
        part_rows(width, offset),
        part_rows(width, offset),
    ]


def backward(s, heads, offset, steps, qkv, probs, go, x0, ga, wqkv, gain1):
    width = s.width
    size = steps * ROWS
    return pl.pallas_call(
        functools.partial(backward_kernel, s, heads),
        grid=(steps,),
        in_specs=row_inputs(s, offset) + [whole(wqkv), whole(gain1)],
        out_specs=[across(ROWS, 3 * width), across(ROWS, width), fixed(1, width)],
        out_shape=[shape((size, 3 * width), BF16), shape((size, width), BF16), shape((1, width), F32)],
        compiler_params=params(60),
        cost_estimate=cost(8e9 * steps, 6e6 * steps),
    )(qkv, probs, go, x0, ga, wqkv, gain1)


def position_grads(s, keep_ref, g0, picked):
    hot_hi, hot_lo = [], []
    for t in range(s.tiles):
        row = keep_ref[t : t + 1, :]
        patches = s.hi_patches if t < s.hi_each else s.lo_patches
        hot = jnp.where(iota((patches, LANES), 0) == row, 1.0, 0.0).astype(BF16)
        (hot_hi if t < s.hi_each else hot_lo).append(hot)
    hi_rows = s.hi_each * LANES
    hi = nn(jnp.concatenate(hot_hi, axis=1), g0[:hi_rows])
    lo = nn(jnp.concatenate(hot_lo, axis=1), g0[hi_rows:])
    return lo, hi, nn(jnp.concatenate(picked, axis=0), g0)


def finish_kernel(s, far, chunks, ids_ref, keep_ref, a_ref, r0_ref, r1_ref, ga_ref, gb_ref, la_ref, lb_ref, p0, p1, p2, p3, w0, w1, w2, w3, q0, q1, q2, q3, o0_ref, o1_ref, e0_ref, e1_ref, i0, i1, i2, i3, turned_ref, acc_ref, lo_ref, hi_ref):
    step = pl.program_id(0)
    width = s.width
    block = width // (8 * far)
    half = width // 2
    done = r0_ref.shape[0]

    @pl.when(step == 0)
    def _():
        turn_relative(ids_ref, far, block, a_ref, turned_ref, acc_ref)

    @pl.when(step < chunks)
    def _():
        value = nn(turned_ref[:, :done], r0_ref[...]) + nn(turned_ref[:, done:], r1_ref[...])
        o0_ref[0] = value[:half].astype(BF16)
        o1_ref[0] = value[half:].astype(BF16)

    @pl.when(step == chunks)
    def _():
        g0 = jnp.concatenate([ga_ref[...], gb_ref[...]], axis=0)
        lo, hi, embed = position_grads(s, keep_ref, g0, [p[...] for p in (p0, p1, p2, p3)])
        lo_ref[...] = lo
        hi_ref[...] = hi
        acc_ref[: s.groups * s.features, :] = embed
        spread_features(s, ids_ref, acc_ref, (e0_ref, e1_ref))
        for weight, pred, out in zip((w0, w1, w2, w3), (q0, q1, q2, q3), (i0, i1, i2, i3)):
            out[: s.features, :] = nt(weight[: s.features, :], g0).astype(BF16)
            out[s.features :, :] = pred[...]
        hi_block = s.hi_patches // (8 * far)
        lo_block = s.lo_patches // (8 * far)
        gain = la_ref[...] + lb_ref[...]
        pad = jnp.zeros((block - hi_block - lo_block - 1, width), F32)
        order = places(ids_ref, far)
        for p in range(0, len(order), 2):
            pair = []
            for at in order[p : p + 2]:
                both = lo_ref[pl.ds(pl.multiple_of((at >> 1) * 8, 8), 8), :]
                pair += [
                    hi_ref[pl.ds(pl.multiple_of(at * hi_block, 8), hi_block), :],
                    jnp.where((at & 1) == 1, both[lo_block:], both[:lo_block]),
                    gain,
                    pad,
                ]
            row = (p % (len(order) // 2)) * block
            (o0_ref, o1_ref)[p // (len(order) // 2)][0, row : row + 2 * block, :] = jnp.concatenate(pair, axis=0).astype(BF16)


def finish(s, ids, far, keep, a, gqkvs, g0s, gains, picked, weights, preds):
    width, rows = s.width, s.rows
    chunks = gqkvs[0].shape[1] // width
    rest = [*g0s, *gains, *picked, *weights, *preds]
    out = pl.BlockSpec((1, width // 2, width), lambda i, ids: (i, 0, 0))
    return pl.pallas_call(
        functools.partial(finish_kernel, s, far, chunks),
        grid_spec=pltpu.PrefetchScalarGridSpec(
            num_scalar_prefetch=1,
            grid=(chunks + 1,),
            in_specs=[whole(keep), whole(a)]
            + [
                pl.BlockSpec((g.shape[0], width), lambda i, ids: (0, jnp.minimum(i, chunks - 1)))
                for g in gqkvs
            ]
            + [whole(r) for r in rest],
            out_specs=[out, out]
            + [fixed(2, 2, s.features // 2, width)] * 2
            + [fixed(2 * s.features, rows)] * 4,
            scratch_shapes=[
                pltpu.VMEM((width, rows), BF16),
                pltpu.VMEM((width, width), F32),
                pltpu.VMEM((s.lo_patches, width), F32),
                pltpu.VMEM((s.hi_patches, width), F32),
            ],
        ),
        out_shape=[shape((chunks + 1, width // 2, width), BF16)] * 2
        + [shape((2, 2, s.features // 2, width), BF16)] * 2
        + [shape((2 * s.features, rows), BF16)] * 4,
        compiler_params=params(60),
        cost_estimate=cost(7e9, 1.2e7),
    )(ids, keep, a, *gqkvs, *rest)


def combine_kernel(held_ref, got_ref, keep_ref, send_ref):
    send_ref[...] = (held_ref[:, 1].astype(F32) + got_ref[:, 1].astype(F32)).astype(BF16)
    keep_ref[...] = (held_ref[:, 0].astype(F32) + got_ref[:, 0].astype(F32)).astype(BF16)


def combine(held, got, axis):
    dims = held.shape
    width = dims[-1]
    outer = math.prod(dims[:axis])
    inner = math.prod(dims[axis + 1 : -1])
    grid = (outer // 4, 1) if outer > 4 else (1, 2)
    broad, tall = outer // grid[0], inner // grid[1]
    half = shape((outer, inner, width), BF16)
    spec = pl.BlockSpec((broad, 2, tall, width), lambda i, j: (i, 0, j, 0))
    out = pl.BlockSpec((broad, tall, width), lambda i, j: (i, j, 0))
    keep, send = pl.pallas_call(
        combine_kernel,
        grid=grid,
        in_specs=[spec, spec],
        out_specs=[out, out],
        out_shape=[half, half],
        compiler_params=params(60),
        cost_estimate=cost(1e6, 6 * outer * inner * width),
    )(*(value.reshape(outer, 2, inner, width) for value in (held, got)))
    left = dims[:axis] + dims[axis + 1 :]
    return keep.reshape(left), send.reshape(left)


def place_kernel(s, member_ref, keep_ref, r0, r1, r2, r3, lo_ref, hi_ref, pred_lo_ref, pred_hi_ref):
    lane_sample = iota((1, LANES), 1) // s.lo_length
    eye = jnp.where(iota((s.features, s.features), 0) == iota((s.features, s.features), 1), 1.0, 0.0).astype(BF16)
    for k, got_ref in enumerate((r0, r1, r2, r3)):
        other = member_ref[0] ^ k
        for i in range(s.hi_each):
            chosen = iota((s.hi_patches, LANES), 0) == keep_ref[k, i : i + 1, :]
            hot = jnp.where(chosen, 1.0, 0.0).astype(BF16)
            lanes = slice(i * LANES, (i + 1) * LANES)
            hi_ref[other * s.hi_each + i] = nt(got_ref[: s.features, lanes], hot).astype(BF16)
            pred_hi_ref[other * s.hi_each + i] = got_ref[s.features :, lanes]
        for tile, first, count in sample_tiles(s):
            lanes = slice(tile * LANES, (tile + 1) * LANES)
            got = got_ref[: s.features, lanes]
            for j in range(count):
                row = jnp.where(lane_sample == j, keep_ref[k, tile : tile + 1, :], -1)
                hot = jnp.where(iota((s.lo_patches, LANES), 0) == row, 1.0, 0.0).astype(BF16)
                lo_ref[other * s.lo_each + first + j] = nt(got, hot).astype(BF16)
            if count:
                size = count * s.lo_length
                turned = tn(got_ref[s.features :, lanes], eye).astype(BF16)
                start = pl.multiple_of((other * s.lo_each + first) * s.lo_length, s.lo_length)
                pred_lo_ref[pl.ds(start, size), :] = turned[:size]


def place(s, member, keep, blocks):
    lo = s.groups * s.lo_each
    hi = s.groups * s.hi_each
    outs = [
        (lo, s.features, s.lo_patches),
        (hi, s.features, s.hi_patches),
        (lo * s.lo_length, s.features),
        (hi, s.features, s.hi_length),
    ]
    return pl.pallas_call(
        functools.partial(place_kernel, s),
        grid_spec=pltpu.PrefetchScalarGridSpec(
            num_scalar_prefetch=1,
            grid=(1,),
            in_specs=[whole(keep)] + [whole(b) for b in blocks],
            out_specs=[fixed(*dims) for dims in outs],
        ),
        out_shape=[shape(dims, BF16) for dims in outs],
        compiler_params=params(60),
        cost_estimate=cost(2e9, 8e6),
    )(member, keep, *blocks)


def swap(value, data_bit, var_bit):
    dp, var = lax.axis_size("dp"), lax.axis_size("var")
    pairs = [
        (d * var + v, (d ^ data_bit) * var + (v ^ var_bit)) for d in range(dp) for v in range(var)
    ]
    return lax.ppermute(value, AXES, pairs)


def add_rounded(left, right):
    return (left.astype(F32) + right.astype(F32)).astype(BF16)


def added(*values):
    values = [value.astype(F32) for value in values]
    while len(values) > 1:
        values = [values[i] + values[i + 1] for i in range(0, len(values), 2)]
    return values[0]


def tie(value, *tokens):
    return lax.optimization_barrier((value, tokens))[0]


PARTNERS = {"core": (0, 1), "x": (0, 2), "y": (1, 0), "z0": (2, 0), "z1": (4, 0)}


class Chain:
    def __init__(self, near, sent):
        self.near, self.sent = near, sent
        self.repeats = near.ndim == 4
        self.names = ["x", "y"] if self.repeats else ["chunk", "x", "y", "z1", "z0"][7 - near.ndim :]
        self.held = self.got = None

    def outgoing(self, name):
        if name == "core":
            self.held = self.near
            return self.sent
        if name not in self.names:
            self.held = add_rounded(self.held, self.got)
            return self.held
        axis = self.names.index(name)
        self.names.remove(name)
        if math.prod(self.held.shape) >= 1 << 20:
            self.held, sent = combine(self.held, self.got, axis)
            return sent
        kept, sent = (
            [lax.index_in_dim(value, side, axis, keepdims=False) for value in (self.held, self.got)]
            for side in range(2)
        )
        self.held = add_rounded(*kept)
        return add_rounded(*sent)

    def hold(self, *tokens):
        self.held, self.got = tie((self.held, self.got), *tokens)

    def final(self):
        return added(self.held, self.got)


def send_rows(values, bits):
    width = values[0].shape[-1]
    if len(values) == 1:
        return [swap(values[0].reshape(-1, width), *bits).reshape(values[0].shape)]
    flat = [value.reshape(-1, width) for value in values]
    got = swap(jnp.concatenate(flat, axis=0), *bits)
    out, start = [], 0
    for value, rows in zip(values, flat):
        out.append(got[start : start + rows.shape[0]].reshape(value.shape))
        start += rows.shape[0]
    return out


def trade(name, *chains):
    got = send_rows([chain.outgoing(name) for chain in chains], PARTNERS[name])
    for chain, value in zip(chains, got):
        chain.got = value
    return got[0]


def both_halves(value):
    value = value.astype(BF16)
    other = swap(value, 1, 0)
    second = lax.axis_index("dp") % 2 == 1
    return jnp.concatenate(
        [jnp.where(second, other, value), jnp.where(second, value, other)], axis=0
    ).astype(F32)


def natural(near, sent):
    rows, width = near.shape[-2:]
    both = jnp.stack([near, sent]).reshape((2, -1, 2, 2, 4, rows, width))
    return both.transpose(4, 3, 2, 0, 1, 5, 6).reshape(32, -1, width)


def scattered(full):
    return lax.psum_scatter(full, AXES, scatter_dimension=0, tiled=True).astype(F32)


def joined(blocks, chunks):
    count, rows, width = blocks.shape
    split = blocks.reshape(count, chunks, rows // chunks, width).transpose(0, 2, 1, 3)
    return split.reshape(count * (rows // chunks), chunks * width)


def plain_sum(near, sent):
    if near.ndim >= 6:
        return natural(near, sent)
    value = jnp.stack([near, sent], axis=1)
    value = value.reshape((4, -1, near.shape[-1]))
    bit = 1
    while value.shape[0] > 1:
        value = value.reshape((value.shape[0] // 2, 2) + value.shape[1:])
        value = add_rounded(value[:, 0], swap(value[:, 1], 0, bit))
        bit *= 2
    return lax.psum(value[0], "dp").astype(F32)


def exchange_relative(blocks):
    return [blocks[0]] + [swap(blocks[k], 0, k) for k in range(1, len(blocks))]


def body(
    img_lo,
    img_hi,
    keep_lo,
    keep_hi,
    mask_lo,
    mask_hi,
    w_embed,
    pos_lo,
    pos_hi,
    ln1_gain,
    w_qkv,
    w_out,
    ln2_gain,
    w_fc1,
    b_fc1,
    w_fc2,
    b_fc2,
    w_head,
    cot_lo,
    cot_hi,
):
    groups = lax.axis_size("var")
    devices = lax.axis_size("dp") * groups
    member = lax.axis_index("var").astype(jnp.int32).reshape(1)
    s = Sizes(keep_lo.shape, keep_hi.shape, w_embed.shape, img_lo.shape, img_hi.shape, groups)
    features, width = s.features, s.width
    gain1, gain2 = ln1_gain.reshape(1, -1), ln2_gain.reshape(1, -1)
    img_lo_t, img_hi_t = img_lo.transpose(0, 2, 1), img_hi.transpose(0, 2, 1)

    own = jnp.concatenate([w_embed, w_head.T], axis=0)
    crossed = swap(own, 0, 2)
    weights = [own, swap(own, 0, 1), crossed, swap(crossed, 0, 1)]
    sent = pick(s, (1, 2, 3), member, keep_lo, keep_hi, img_lo_t, img_hi_t)
    picked = [swap(value, 0, k + 1) for k, value in enumerate(sent)]
    picked = [*pick(s, (0,), member, keep_lo, keep_hi, img_lo_t, img_hi_t), *picked]
    keep, seen, *cots = stage(
        s,
        tie(member, sent[0]),
        keep_lo,
        keep_hi,
        mask_lo,
        mask_hi,
        cot_lo.reshape(-1, features),
        cot_hi.transpose(0, 2, 1),
    )
    cots = exchange_relative(cots)
    own_keep = keep[0]
    x0, a, qkv, probs, mixed, x1 = forward(
        s, HEADS, own_keep, seen, picked, weights, pos_lo, pos_hi, gain1, w_qkv, w_out
    )
    far = 4
    cube = lax.axis_size("dp") == 2 * far
    place_of = lax.axis_index("dp") * groups + lax.axis_index("var")
    ids = jnp.stack([lax.axis_index("dp"), lax.axis_index("var")]).astype(jnp.int32)
    if not cube:
        ids = jnp.zeros_like(ids)

    def chain_of(near, sent):
        if near.ndim == 5:
            near, sent = (
                value.reshape((2, 2, 2, 2) + value.shape[3:]) for value in (near, sent)
            )
        elif near.ndim == 3:
            near, sent = (
                value.reshape((-1, 2, 2, 2, 2, width // 32, width)) for value in (near, sent)
            )
        return Chain(near, sent)

    def step(name, *chains):
        return trade(name, *chains) if cube else ()

    def halves_of(chain):
        out = []
        for side in range(2):
            piece = Chain(chain.near, chain.sent)
            count = chain.near.shape[0] // 2
            piece.held, piece.got = (
                lax.slice_in_dim(value, side * count, (side + 1) * count, axis=0)
                for value in (chain.held, chain.got)
            )
            out.append(piece)
        return out

    two0, two1, one0, one1, *rest = hidden(
        s,
        ids,
        far,
        tie(seen, x1),
        cots,
        weights,
        x1,
        mixed,
        w_fc1,
        b_fc1.reshape(1, -1),
        w_fc2,
        b_fc2.reshape(1, -1),
        gain2,
        w_out,
    )
    preds, (out0, out1, head0, head1, go, ga) = rest[:groups], rest[groups:]
    two, one = chain_of(two0, two1), chain_of(one0, one1)
    out, head = chain_of(out0, out1), chain_of(head0, head1)
    tokens = [step("core", chain) for chain in (two, one, out, head)]

    def back(offset, steps, *ready):
        return backward(
            s, HEADS, offset, steps, qkv, probs, go, x0, ga, w_qkv, tie(gain1, *ready)
        )

    parts = [back(0, 1, go)]
    if cube:
        for chain in (two, one, out, head):
            chain.hold(parts[0][0])
    near_tokens = [step("x", two, out, head), step("y", one)]
    parts.append(back(1, s.rows // ROWS - 1, parts[0][0], two.held, one.held, *tokens))
    if cube:
        for chain in (two, one, out, head):
            chain.hold(parts[1][0])
    tokens = [step("y", two, out, head), step("x", one)]
    gqkvs, g0s, gains = zip(*parts)
    near, sent, near_embed, sent_embed, *blocks = finish(
        s,
        tie(ids, two.held, one.held, *near_tokens),
        far,
        own_keep,
        a,
        gqkvs,
        g0s,
        gains,
        picked,
        weights,
        preds,
    )
    sent, sent_embed = tie((sent, sent_embed), *tokens)
    first, embed = chain_of(near, sent), chain_of(near_embed, sent_embed)
    tokens += [step("core", first), step("core", embed)]
    if cube:
        old = (two, one, out, head)
        for chain in old:
            chain.hold(first.got)
        one_half, other_half = halves_of(first)
        tokens = [trade("x", one_half, embed), trade("y", other_half)]
        trade("z0", *old)
        for chain in old:
            chain.hold(*tokens)
        tokens = [trade("y", one_half, embed), trade("x", other_half)]
        trade("z1", *old)
        blocks = [tie(block_of, *tokens) for block_of in blocks]
        trade("z0", one_half, other_half, embed)
        token = trade("z1", one_half, other_half, embed)
        for chain in old:
            chain.hold(token)
        last_member = tie(member, token)
        grad_fc2, grad_fc1, rest, grad_head, grad_embed = (
            chain.final() for chain in (two, one, out, head, embed)
        )
        grad_head, grad_embed = both_halves(grad_head), both_halves(grad_embed)
        first = jnp.concatenate([one_half.final(), other_half.final()], axis=0).reshape(-1, width)
        grad_fc1 = grad_fc1.reshape(-1, width)
    else:
        grad_fc2, grad_fc1, rest, grad_head, grad_embed, first = (
            plain_sum(chain.near, chain.sent) for chain in (two, one, out, head, embed, first)
        )
        last_member = member
    grad_img_lo, grad_img_hi, pred_lo, pred_hi = place(s, last_member, keep, exchange_relative(blocks))
    grad_head = grad_head.T

    block = width // devices
    inner = w_fc1.shape[1] // width

    hi_block = s.hi_patches // devices
    lo_block = s.lo_patches // devices

    def own_part(row):
        return lax.dynamic_slice_in_dim(row, place_of * block, block)

    if cube:
        grad_fc1 = joined(grad_fc1[None], inner)
        grad_qkv = joined(first[None, : 3 * block], 3)
        grad_out, sides = rest[:block], rest[block:]
        extra = first[3 * block :]
        grad_pos_hi = extra[:hi_block]
        grad_pos_lo = extra[hi_block : hi_block + lo_block]
        first_side = extra[hi_block + lo_block]
    else:
        tall = width // 32
        hi_tall, lo_tall = s.hi_patches // 32, s.lo_patches // 32
        grad_fc2 = scattered(grad_fc2.reshape(-1, width))
        grad_fc1 = scattered(joined(grad_fc1, inner))
        grad_qkv = scattered(joined(first[:, : 3 * tall], 3))
        grad_out, sides = scattered(rest[:, :tall].reshape(-1, width)), rest[0, tall:]
        extra = first[:, 3 * tall :]
        grad_pos_hi = scattered(extra[:, :hi_tall].reshape(-1, width))
        grad_pos_lo = scattered(extra[:, hi_tall : hi_tall + lo_tall].reshape(-1, width))
        sides = lax.psum(jnp.concatenate([sides, extra[0, hi_tall + lo_tall :]]), AXES).astype(F32)
        first_side = sides[rest.shape[1] - tall]
    grad_ln1 = own_part(first_side)
    grad_ln2 = own_part(sides[0])
    grad_b2 = own_part(sides[1])
    grad_b1 = lax.dynamic_slice_in_dim(
        sides[2 : 2 + inner].reshape(-1), place_of * inner * block, inner * block
    )
    return (
        pred_lo.reshape(cot_lo.shape),
        pred_hi.transpose(0, 2, 1),
        grad_img_lo.transpose(0, 2, 1),
        grad_img_hi.transpose(0, 2, 1),
        grad_embed,
        grad_pos_lo,
        grad_pos_hi,
        grad_ln1,
        grad_qkv,
        grad_out,
        grad_ln2,
        grad_fc1,
        grad_b1,
        grad_fc2,
        grad_b2,
        grad_head,
    )


def solution(mesh):
    placed = (
        P("dp", None, "var"),
        P("dp", None, "var"),
        P("dp", None),
        P("dp", None),
        P("dp", None),
        P("dp", None),
        P("var", None),
        P(),
        P(),
        P(),
        P(),
        P(),
        P(),
        P(),
        P(),
        P(),
        P(),
        P(None, "var"),
        P("dp", None, "var"),
        P("dp", None, "var"),
    )
    return jax.shard_map(
        body,
        mesh=mesh,
        in_specs=placed,
        out_specs=(
            P("dp", None, "var"),
            P("dp", None, "var"),
            P("dp", None, "var"),
            P("dp", None, "var"),
            P("var", None),
            P(("dp", "var"), None),
            P(("dp", "var"), None),
            P(("dp", "var")),
            P(("dp", "var"), None),
            P(("dp", "var"), None),
            P(("dp", "var")),
            P(("dp", "var"), None),
            P(("dp", "var")),
            P(("dp", "var"), None),
            P(("dp", "var")),
            P(None, "var"),
        ),
        check_vma=False,
    )
```

profile of v0, /device:TPU:0, one launch (start us, length us, event | category | flops | bytes accessed | tf_op | source)
XLA Modules:
  0.0 254.2 jit_solution(14475326519697476858)
XLA Ops:
  1.6 3.0 %collective-permute-start.4 = (bf16[160,768]{1,0:T(8,128)(2,1)S(1)}, bf16[160,768]{1,0:T(8,128)(2,1)S(1)}, u32[]{:S(2)}, u32[]{:S(2)}) collective-permute-start(bf16[160,768]{1,0:T(8,128)(2,1)S(1)} %pad_maximum_fusion.7.w0.h0), channel_id=1, source_target_pairs={{0,2},{1,3},{2,0},{3,1},{4,6},{5,7},{6,4},{7,5},{8,10},{9,11},{10,... | collective-permute-start | bytes 737288 | tf_op jit(solution)/shard_map/ppermute | solution.py:738
  6.1 3.3 %shard_map.315 = (bf16[80,1024]{1,0:T(8,128)(2,1)}, bf16[80,1024]{1,0:T(8,128)(2,1)}, bf16[80,1024]{1,0:T(8,128)(2,1)}) custom-call(s32[1]{0:T(128)} %bitcast.member_ref, s32[40,32]{1,0:T(8,128)} %copy.92.keep_lo_ref, s32[20,128]{1,0:T(8,128)} %keep_hi_ref.5, bf16[40,80,128]{2,1,0:T(8,128)(2,1)} %bitcast.250, bf16[20,80,512]{2,1,0:T(8,128)(2,1)} %bitcast.247), custom_call_target="tpu_custom_call" | custom-call | flops 1000000000 | bytes 2000000 | tf_op jit(solution)/shard_map/pallas_call | solution.py:158
  12.0 2.3 shard_map.316
  18.1 2.9 %shard_map.317.p0 = bf16[80,1024]{1,0:T(8,128)(2,1)} custom-call(s32[1]{0:T(128)} %bitcast.member_ref, s32[40,32]{1,0:T(8,128)} %copy.92.keep_lo_ref, s32[20,128]{1,0:T(8,128)} %keep_hi_ref.5, bf16[40,80,128]{2,1,0:T(8,128)(2,1)} %bitcast.251, bf16[20,80,512]{2,1,0:T(8,128)(2,1)} %bitcast.248), custom_call_target="tpu_custom_call" | custom-call | flops 1000000000 | bytes 2000000 | tf_op jit(solution)/shard_map/pallas_call | solution.py:158
  24.5 19.2 %shard_map.318 = (bf16[1024,768]{1,0:T(8,128)(2,1)}, bf16[1024,768]{1,0:T(8,128)(2,1)}, bf16[1024,2304]{1,0:T(8,128)(2,1)}, bf16[8,6,256,128]{3,2,1,0:T(8,128)(2...) custom-call(s32[8,128]{1,0:T(8,128)} %slice_bitcast_fusion.6.keep_ref, f32[8,128]{1,0:T(8,128)} %get-tuple-element.126.seen_ref, ...), custom_call_target="tpu_custom_call" | custom-call | flops 7500000256 | bytes 15000000 | tf_op jit(solution)/shard_map/pallas_call | solution.py:285
  44.4 54.8 %shard_map.319 = (bf16[2,2,4,96,768]{4,3,2,1,0:T(8,128)(2,1)}, bf16[2,2,4,96,768]{4,3,2,1,0:T(8,128)(2,1)}, bf16[4,384,768]{2,1,0:T(8,128)(2,1)}, bf16[4,384,768...) custom-call(s32[2]{0:T(128)} %pad_add_fusion.ids_ref, ...), custom_call_target="tpu_custom_call" | custom-call | flops 16999999488 | bytes 20000000 | tf_op jit(solution)/shard_map/pallas_call | solution.py:469
  100.3 8.8 %shard_map.320 = (bf16[256,2304]{1,0:T(8,128)(2,1)}, bf16[256,768]{1,0:T(8,128)(2,1)}, f32[1,768]{1,0:T(1,128)}) custom-call(bf16[1024,2304]{1,0:T(8,128)(2,1)} %get-tuple-element.134.qkv_ref, bf16[8,6,256,128]{3,2,1,0:T(8,128)(2,1)} %get-tuple-element.135.probs_ref, bf16[1024,768]{1,0:T(8,128)(2,1)} %get-tuple-element.136.go_ref, ...), custom_call_target="tpu_custom_call" | custom-call | flops 4000000000 | bytes 3000000 | tf_op jit(solution)/shard_map/pallas_call | solution.py:552
  111.0 3.6 %shard_map.321 = (bf16[1,768,768]{2,1,0:T(8,128)(2,1)}, bf16[1,768,768]{2,1,0:T(8,128)(2,1)}) custom-call(bf16[1,2,768,768]{3,2,1,0:T(8,128)(2,1)} %bitcast.194, bf16[1,2,768,768]{3,2,1,0:T(8,128)(2,1)} %bitcast.13.got_ref), custom_call_target="tpu_custom_call" | custom-call | flops 500000 | bytes 1769472 | tf_op jit(solution)/shard_map/pallas_call | solution.py:672
  114.6 2.6 %pad_maximum_fusion = bf16[1104,768]{1,0:T(8,128)(2,1)} fusion(bf16[80,768]{1,0:T(8,128)(2,1)S(1)} %bitcast.228, bf16[256,768]{1,0:T(8,128)(2,1)S(1)} %bitcast.198, bf16[768,768]{1,0:T(8,128)(2,1)} %bitcast.204), kind=kLoop, calls=%fused_computation | loop fusion | flops 5087232 | bytes 3391488 | tf_op jit(solution)/shard_map/concatenate | solution.py:797
  119.0 3.6 %shard_map.322 = (bf16[8,96,768]{2,1,0:T(8,128)(2,1)}, bf16[8,96,768]{2,1,0:T(8,128)(2,1)}) custom-call(bf16[8,2,96,768]{3,2,1,0:T(8,128)(2,1)} %bitcast.193, bf16[8,2,96,768]{3,2,1,0:T(8,128)(2,1)} %bitcast.195), custom_call_target="tpu_custom_call" | custom-call | flops 500000 | bytes 1769472 | tf_op jit(solution)/shard_map/pallas_call | solution.py:672
  125.5 20.0 %shard_map.323 = (bf16[768,2304]{1,0:T(8,128)(2,1)}, bf16[768,768]{1,0:T(8,128)(2,1)}, f32[1,768]{1,0:T(1,128)}) custom-call(bf16[1024,2304]{1,0:T(8,128)(2,1)} %get-tuple-element.134.qkv_ref, bf16[8,6,256,128]{3,2,1,0:T(8,128)(2,1)} %get-tuple-element.135.probs_ref, bf16[1024,768]{1,0:T(8,128)(2,1)} %get-tuple-element.136.go_ref, ...), custom_call_target="tpu_custom_call" | custom-call | flops 12000000000 | bytes 9000000 | tf_op jit(solution)/shard_map/pallas_call | solution.py:552
  145.5 5.2 %collective-permute-done.14 = bf16[768,768]{1,0:T(8,128)(2,1)S(1)} collective-permute-done((bf16[768,768]{1,0:T(8,128)(2,1)}, bf16[768,768]{1,0:T(8,128)(2,1)S(1)}, u32[]{:S(2)}, u32[]{:S(2)}) %collective-permute-start.14) | collective-permute-done | bytes 1179680 | tf_op jit(solution)/shard_map/ppermute | solution.py:738
  150.7 5.9 %collective-permute-done.12 = bf16[1104,768]{1,0:T(8,128)(2,1)S(1)} collective-permute-done((bf16[1104,768]{1,0:T(8,128)(2,1)}, bf16[1104,768]{1,0:T(8,128)(2,1)S(1)}, u32[]{:S(2)}, u32[]{:S(2)}) %collective-permute-start.12) | collective-permute-done | bytes 1695776 | tf_op jit(solution)/shard_map/ppermute | solution.py:738
  161.7 14.4 %shard_map.324 = (bf16[4,384,768]{2,1,0:T(8,128)(2,1)}, bf16[4,384,768]{2,1,0:T(8,128)(2,1)}, bf16[2,2,40,768]{3,2,1,0:T(8,128)(2,1)}, bf16[2,2,40,768]{3,2,1,0:...) custom-call(s32[2]{0:T(128)} %pad_add_fusion.ids_ref, ...), custom_call_target="tpu_custom_call" | custom-call | flops 3500000000 | bytes 6000000 | tf_op jit(solution)/shard_map/pallas_call | solution.py:628
  176.0 3.2 %collective-permute-done.15 = bf16[552,768]{1,0:T(8,128)(2,1)S(1)} collective-permute-done((bf16[552,768]{1,0:T(8,128)(2,1)S(1)}, bf16[552,768]{1,0:T(8,128)(2,1)S(1)}, u32[]{:S(2)}, u32[]{:S(2)}) %collective-permute-start.15) | collective-permute-done | bytes 847904 | tf_op jit(solution)/shard_map/ppermute | solution.py:738
  181.7 2.1 collective-permute-done.18
  190.5 10.3 %collective-permute-done.21 = bf16[384,768]{1,0:T(8,128)(2,1)S(1)} collective-permute-done((bf16[384,768]{1,0:T(8,128)(2,1)S(1)}, bf16[384,768]{1,0:T(8,128)(2,1)S(1)}, u32[]{:S(2)}, u32[]{:S(2)}) %collective-permute-start.21) | collective-permute-done | bytes 589856 | tf_op jit(solution)/shard_map/ppermute | solution.py:738
  205.0 2.0 collective-permute-done.29
  207.3 2.6 %collective-permute-start.30 = (bf16[264,768]{1,0:T(8,128)(2,1)S(1)}, bf16[264,768]{1,0:T(8,128)(2,1)S(1)}, u32[]{:S(2)}, u32[]{:S(2)}) collective-permute-start(bf16[264,768]{1,0:T(8,128)(2,1)S(1)} %pad_maximum_fusion.4), channel_id=1, source_target_pairs={{0,16},{1,17},{2,18},{3,19},{4,20},{5,21},{6,22},{7,23},{8,24},{9,... | collective-permute-start | bytes 1216520 | tf_op jit(solution)/shard_map/ppermute | solution.py:738
  210.0 2.8 %collective-permute-done.20 = bf16[232,768]{1,0:T(8,128)(2,1)S(1)} collective-permute-done((bf16[232,768]{1,0:T(8,128)(2,1)S(1)}, bf16[232,768]{1,0:T(8,128)(2,1)S(1)}, u32[]{:S(2)}, u32[]{:S(2)}) %collective-permute-start.20) | collective-permute-done | bytes 356384 | tf_op jit(solution)/shard_map/ppermute | solution.py:738
  216.5 10.4 %collective-permute-done.30 = bf16[264,768]{1,0:T(8,128)(2,1)S(1)} collective-permute-done((bf16[264,768]{1,0:T(8,128)(2,1)S(1)}, bf16[264,768]{1,0:T(8,128)(2,1)S(1)}, u32[]{:S(2)}, u32[]{:S(2)}) %collective-permute-start.30) | collective-permute-done | bytes 405536 | tf_op jit(solution)/shard_map/ppermute | solution.py:738
  229.1 2.9 %collective-permute-start.24 = (bf16[136,768]{1,0:T(8,128)(2,1)S(1)}, bf16[136,768]{1,0:T(8,128)(2,1)S(1)}, u32[]{:S(2)}, u32[]{:S(2)}) collective-permute-start(bf16[136,768]{1,0:T(8,128)(2,1)S(1)} %pad_maximum_fusion.9), channel_id=1, source_target_pairs={{0,16},{1,17},{2,18},{3,19},{4,20},{5,21},{6,22},{7,23},{8,24},{9,... | collective-permute-start | bytes 626696 | tf_op jit(solution)/shard_map/ppermute | solution.py:738
  232.0 7.4 %collective-permute-done.24 = bf16[136,768]{1,0:T(8,128)(2,1)S(1)} collective-permute-done((bf16[136,768]{1,0:T(8,128)(2,1)S(1)}, bf16[136,768]{1,0:T(8,128)(2,1)S(1)}, u32[]{:S(2)}, u32[]{:S(2)}) %collective-permute-start.24) | collective-permute-done | bytes 208928 | tf_op jit(solution)/shard_map/ppermute | solution.py:738
  247.9 4.6 %shard_map.325 = (bf16[40,80,128]{2,1,0:T(8,128)(2,1)}, bf16[20,80,512]{2,1,0:T(8,128)(2,1)}, bf16[1280,80]{1,0:T(8,128)(2,1)}, bf16[20,80,128]{2,1,0:T(8,128)(2,1)}) custom-call(s32[1]{0:T(128)} %bitcast.member_ref, s32[4,8,128]{2,1,0:T(8,128)} %get-tuple-element.122.keep_ref, bf16[160,1024]{1,0:T(8,128)(2,1)} %get-tuple-element.187.r0, ...), custom_call_target="tpu_custom_call" | custom-call | flops 1000000000 | bytes 4000000 | tf_op jit(solution)/shard_map/pallas_call | solution.py:719
  (220 shorter events, 54.8 us)
Async XLA Ops:
  1.6 12.6 %collective-permute-start.4 = (bf16[160,768]{1,0:T(8,128)(2,1)S(1)}, bf16[160,768]{1,0:T(8,128)(2,1)S(1)}, u32[]{:S(2)}, u32[]{:S(2)}) collective-permute-start(bf16[160,768]{1,0:T(8,128)(2,1)S(1)} %pad_maximum_fusion.7.w0.h0), channel_id=1, source_target_pairs={{0,2},{1,3},{2,0},{3,1},{4,6},{5,7},{6,4},{7,5},{8,10},{9,11},{10,... | collective-permute-start | bytes 737288 | tf_op jit(solution)/shard_map/ppermute | solution.py:738
  4.6 19.0 %collective-permute-start.3 = (bf16[160,768]{1,0:T(8,128)(2,1)S(1)}, bf16[160,768]{1,0:T(8,128)(2,1)S(1)}, u32[]{:S(2)}, u32[]{:S(2)}) collective-permute-start(bf16[160,768]{1,0:T(8,128)(2,1)S(1)} %pad_maximum_fusion.7.w0.h0), channel_id=1, source_target_pairs={{0,1},{1,0},{2,3},{3,2},{4,5},{5,4},{6,7},{7,6},{8,9},{9,8},{10,11... | collective-permute-start | bytes 737288 | tf_op jit(solution)/shard_map/ppermute | solution.py:738
  9.4 12.2 %collective-permute-start = (bf16[80,1024]{1,0:T(8,128)(2,1)}, bf16[80,1024]{1,0:T(8,128)(2,1)S(1)}, u32[]{:S(2)}, u32[]{:S(2)}) collective-permute-start(bf16[80,1024]{1,0:T(8,128)(2,1)} %get-tuple-element.119), channel_id=1, source_target_pairs={{0,1},{1,0},{2,3},{3,2},{4,5},{5,4},{6,7},{7,6},{8,9},{9,8},{10,11... | collective-permute-start | bytes 491528 | tf_op jit(solution)/shard_map/ppermute | solution.py:738
  9.9 11.8 %collective-permute-start.1 = (bf16[80,1024]{1,0:T(8,128)(2,1)}, bf16[80,1024]{1,0:T(8,128)(2,1)S(1)}, u32[]{:S(2)}, u32[]{:S(2)}) collective-permute-start(bf16[80,1024]{1,0:T(8,128)(2,1)} %get-tuple-element.123), channel_id=1, source_target_pairs={{0,2},{1,3},{2,0},{3,1},{4,6},{5,7},{6,4},{7,5},{8,10},{9,11},{10,... | collective-permute-start | bytes 491528 | tf_op jit(solution)/shard_map/ppermute | solution.py:738
  10.0 12.2 %collective-permute-start.2 = (bf16[80,1024]{1,0:T(8,128)(2,1)}, bf16[80,1024]{1,0:T(8,128)(2,1)S(1)}, u32[]{:S(2)}, u32[]{:S(2)}) collective-permute-start(bf16[80,1024]{1,0:T(8,128)(2,1)} %get-tuple-element.124), channel_id=1, source_target_pairs={{0,3},{1,2},{2,1},{3,0},{4,7},{5,6},{6,5},{7,4},{8,11},{9,10},{10,... | collective-permute-start | bytes 491528 | tf_op jit(solution)/shard_map/ppermute | solution.py:738
  21.6 22.0 %collective-permute-start.6 = (bf16[80,1024]{1,0:T(8,128)(2,1)S(1)}, bf16[80,1024]{1,0:T(8,128)(2,1)S(1)}, u32[]{:S(2)}, u32[]{:S(2)}) collective-permute-start(bf16[80,1024]{1,0:T(8,128)(2,1)S(1)} %copy-done.30), channel_id=1, source_target_pairs={{0,1},{1,0},{2,3},{3,2},{4,5},{5,4},{6,7},{7,6},{8,9},{9,8},{10,11... | collective-permute-start | bytes 491528 | tf_op jit(solution)/shard_map/ppermute | solution.py:738
  21.7 21.9 %collective-permute-start.7 = (bf16[80,1024]{1,0:T(8,128)(2,1)S(1)}, bf16[80,1024]{1,0:T(8,128)(2,1)S(1)}, u32[]{:S(2)}, u32[]{:S(2)}) collective-permute-start(bf16[80,1024]{1,0:T(8,128)(2,1)S(1)} %copy-done.29), channel_id=1, source_target_pairs={{0,2},{1,3},{2,0},{3,1},{4,6},{5,7},{6,4},{7,5},{8,10},{9,11},{10,... | collective-permute-start | bytes 491528 | tf_op jit(solution)/shard_map/ppermute | solution.py:738
  22.2 21.5 %collective-permute-start.8 = (bf16[80,1024]{1,0:T(8,128)(2,1)S(1)}, bf16[80,1024]{1,0:T(8,128)(2,1)S(1)}, u32[]{:S(2)}, u32[]{:S(2)}) collective-permute-start(bf16[80,1024]{1,0:T(8,128)(2,1)S(1)} %copy-done.28), channel_id=1, source_target_pairs={{0,3},{1,2},{2,1},{3,0},{4,7},{5,6},{6,5},{7,4},{8,11},{9,10},{10,... | collective-permute-start | bytes 491528 | tf_op jit(solution)/shard_map/ppermute | solution.py:738
  99.2 11.7 %collective-permute-start.9 = (bf16[1536,768]{1,0:T(8,128)(2,1)}, bf16[1536,768]{1,0:T(8,128)(2,1)}, u32[]{:S(2)}, u32[]{:S(2)}) collective-permute-start(bf16[1536,768]{1,0:T(8,128)(2,1)} %bitcast.246), channel_id=1, source_target_pairs={{0,1},{1,0},{2,3},{3,2},{4,5},{5,4},{6,7},{7,6},{8,9},{9,8},{10,11... | collective-permute-start | bytes 7077896 | tf_op jit(solution)/shard_map/ppermute | solution.py:738
  99.6 17.9 %collective-permute-start.13 = (bf16[1536,768]{1,0:T(8,128)(2,1)}, bf16[1536,768]{1,0:T(8,128)(2,1)S(1)}, u32[]{:S(2)}, u32[]{:S(2)}) collective-permute-start(bf16[1536,768]{1,0:T(8,128)(2,1)} %bitcast.244), channel_id=1, source_target_pairs={{0,1},{1,0},{2,3},{3,2},{4,5},{5,4},{6,7},{7,6},{8,9},{9,8},{10,11... | collective-permute-start | bytes 7077896 | tf_op jit(solution)/shard_map/ppermute | solution.py:738
  117.2 39.4 %collective-permute-start.12 = (bf16[1104,768]{1,0:T(8,128)(2,1)}, bf16[1104,768]{1,0:T(8,128)(2,1)S(1)}, u32[]{:S(2)}, u32[]{:S(2)}) collective-permute-start(bf16[1104,768]{1,0:T(8,128)(2,1)} %pad_maximum_fusion), channel_id=1, source_target_pairs={{0,2},{1,3},{2,0},{3,1},{4,6},{5,7},{6,4},{7,5},{8,10},{9,11},{10,... | collective-permute-start | bytes 5087240 | tf_op jit(solution)/shard_map/ppermute | solution.py:738
  122.5 28.1 %collective-permute-start.14 = (bf16[768,768]{1,0:T(8,128)(2,1)}, bf16[768,768]{1,0:T(8,128)(2,1)S(1)}, u32[]{:S(2)}, u32[]{:S(2)}) collective-permute-start(bf16[768,768]{1,0:T(8,128)(2,1)} %bitcast.249), channel_id=1, source_target_pairs={{0,4},{1,5},{2,6},{3,7},{4,0},{5,1},{6,2},{7,3},{8,12},{9,13},{10,... | collective-permute-start | bytes 3538952 | tf_op jit(solution)/shard_map/ppermute | solution.py:738
  159.0 20.3 %collective-permute-start.15 = (bf16[552,768]{1,0:T(8,128)(2,1)S(1)}, bf16[552,768]{1,0:T(8,128)(2,1)S(1)}, u32[]{:S(2)}, u32[]{:S(2)}) collective-permute-start(bf16[552,768]{1,0:T(8,128)(2,1)S(1)} %pad_maximum_fusion.1), channel_id=1, source_target_pairs={{0,4},{1,5},{2,6},{3,7},{4,0},{5,1},{6,2},{7,3},{8,12},{9,13},{10,... | collective-permute-start | bytes 2543624 | tf_op jit(solution)/shard_map/ppermute | solution.py:738
  160.9 18.4 %collective-permute-start.16 = (bf16[384,768]{1,0:T(8,128)(2,1)S(1)}, bf16[384,768]{1,0:T(8,128)(2,1)S(1)}, u32[]{:S(2)}, u32[]{:S(2)}) collective-permute-start(bf16[384,768]{1,0:T(8,128)(2,1)S(1)} %bitcast.217), channel_id=1, source_target_pairs={{0,2},{1,3},{2,0},{3,1},{4,6},{5,7},{6,4},{7,5},{8,10},{9,11},{10,... | collective-permute-start | bytes 1769480 | tf_op jit(solution)/shard_map/ppermute | solution.py:738
  184.9 18.4 %collective-permute-start.19 = (bf16[464,768]{1,0:T(8,128)(2,1)S(1)}, bf16[464,768]{1,0:T(8,128)(2,1)S(1)}, u32[]{:S(2)}, u32[]{:S(2)}) collective-permute-start(bf16[464,768]{1,0:T(8,128)(2,1)S(1)} %pad_maximum_fusion.3), channel_id=1, source_target_pairs={{0,2},{1,3},{2,0},{3,1},{4,6},{5,7},{6,4},{7,5},{8,10},{9,11},{10,... | collective-permute-start | bytes 2138120 | tf_op jit(solution)/shard_map/ppermute | solution.py:738
  185.5 15.2 %collective-permute-start.21 = (bf16[384,768]{1,0:T(8,128)(2,1)S(1)}, bf16[384,768]{1,0:T(8,128)(2,1)S(1)}, u32[]{:S(2)}, u32[]{:S(2)}) collective-permute-start(bf16[384,768]{1,0:T(8,128)(2,1)S(1)} %bitcast.218), channel_id=1, source_target_pairs={{0,4},{1,5},{2,6},{3,7},{4,0},{5,1},{6,2},{7,3},{8,12},{9,13},{10,... | collective-permute-start | bytes 1769480 | tf_op jit(solution)/shard_map/ppermute | solution.py:738
  188.6 18.3 %collective-permute-start.29 = (bf16[488,768]{1,0:T(8,128)(2,1)S(1)}, bf16[488,768]{1,0:T(8,128)(2,1)S(1)}, u32[]{:S(2)}, u32[]{:S(2)}) collective-permute-start(bf16[488,768]{1,0:T(8,128)(2,1)S(1)} %pad_maximum_fusion.2), channel_id=1, source_target_pairs={{0,8},{1,9},{2,10},{3,11},{4,12},{5,13},{6,14},{7,15},{8,0},{9,1},... | collective-permute-start | bytes 2248712 | tf_op jit(solution)/shard_map/ppermute | solution.py:738
  207.3 19.7 %collective-permute-start.30 = (bf16[264,768]{1,0:T(8,128)(2,1)S(1)}, bf16[264,768]{1,0:T(8,128)(2,1)S(1)}, u32[]{:S(2)}, u32[]{:S(2)}) collective-permute-start(bf16[264,768]{1,0:T(8,128)(2,1)S(1)} %pad_maximum_fusion.4), channel_id=1, source_target_pairs={{0,16},{1,17},{2,18},{3,19},{4,20},{5,21},{6,22},{7,23},{8,24},{9,... | collective-permute-start | bytes 1216520 | tf_op jit(solution)/shard_map/ppermute | solution.py:738
  213.0 15.9 %collective-permute-start.23 = (bf16[232,768]{1,0:T(8,128)(2,1)S(1)}, bf16[232,768]{1,0:T(8,128)(2,1)S(1)}, u32[]{:S(2)}, u32[]{:S(2)}) collective-permute-start(bf16[232,768]{1,0:T(8,128)(2,1)S(1)} %pad_maximum_fusion.6), channel_id=1, source_target_pairs={{0,8},{1,9},{2,10},{3,11},{4,12},{5,13},{6,14},{7,15},{8,0},{9,1},... | collective-permute-start | bytes 1069064 | tf_op jit(solution)/shard_map/ppermute | solution.py:738
  214.7 33.3 %collective-permute-start.27 = (bf16[160,1024]{1,0:T(8,128)(2,1)S(1)}, bf16[160,1024]{1,0:T(8,128)(2,1)}, u32[]{:S(2)}, u32[]{:S(2)}) collective-permute-start(bf16[160,1024]{1,0:T(8,128)(2,1)S(1)} %copy-done.20), channel_id=1, source_target_pairs={{0,3},{1,2},{2,1},{3,0},{4,7},{5,6},{6,5},{7,4},{8,11},{9,10},{10,... | collective-permute-start | bytes 983048 | tf_op jit(solution)/shard_map/ppermute | solution.py:738
  214.7 33.3 %collective-permute-start.26 = (bf16[160,1024]{1,0:T(8,128)(2,1)S(1)}, bf16[160,1024]{1,0:T(8,128)(2,1)}, u32[]{:S(2)}, u32[]{:S(2)}) collective-permute-start(bf16[160,1024]{1,0:T(8,128)(2,1)S(1)} %copy-done.19), channel_id=1, source_target_pairs={{0,2},{1,3},{2,0},{3,1},{4,6},{5,7},{6,4},{7,5},{8,10},{9,11},{10,... | collective-permute-start | bytes 983048 | tf_op jit(solution)/shard_map/ppermute | solution.py:738
  215.4 32.6 %collective-permute-start.25 = (bf16[160,1024]{1,0:T(8,128)(2,1)S(1)}, bf16[160,1024]{1,0:T(8,128)(2,1)}, u32[]{:S(2)}, u32[]{:S(2)}) collective-permute-start(bf16[160,1024]{1,0:T(8,128)(2,1)S(1)} %copy-done.18), channel_id=1, source_target_pairs={{0,1},{1,0},{2,3},{3,2},{4,5},{5,4},{6,7},{7,6},{8,9},{9,8},{10,11... | collective-permute-start | bytes 983048 | tf_op jit(solution)/shard_map/ppermute | solution.py:738
  229.1 10.3 %collective-permute-start.24 = (bf16[136,768]{1,0:T(8,128)(2,1)S(1)}, bf16[136,768]{1,0:T(8,128)(2,1)S(1)}, u32[]{:S(2)}, u32[]{:S(2)}) collective-permute-start(bf16[136,768]{1,0:T(8,128)(2,1)S(1)} %pad_maximum_fusion.9), channel_id=1, source_target_pairs={{0,16},{1,17},{2,18},{3,19},{4,20},{5,21},{6,22},{7,23},{8,24},{9,... | collective-permute-start | bytes 626696 | tf_op jit(solution)/shard_map/ppermute | solution.py:738
  241.4 11.1 %collective-permute-start.28 = (bf16[40,768]{1,0:T(8,128)(2,1)S(1)}, bf16[40,768]{1,0:T(8,128)(2,1)S(1)}, u32[]{:S(2)}, u32[]{:S(2)}) collective-permute-start(bf16[40,768]{1,0:T(8,128)(2,1)S(1)} %add_convert_fusion.40), channel_id=1, source_target_pairs={{0,4},{1,5},{2,6},{3,7},{4,0},{5,1},{6,2},{7,3},{8,12},{9,13},{10,... | collective-permute-start | bytes 184328 | tf_op jit(solution)/shard_map/ppermute | solution.py:738
  (47 other events, 211.0 us)
where the time goes:
time: 259 us; the launch traced here: 254 us
  Pallas kernels  137 us (53%)
  waiting for transfers between devices  52.6 us (20%)
  starting transfers between devices  31.8 us (12%)
  local copies, waits for them, and re-layouts  17.9 us (7%)
  other arithmetic  13 us (5%)
    pallas_call x1, Pallas kernels, hidden(): pl.pallas_call(functools.partial(hidden_kernel, s, far, chunks), grid_spe...  54.8 us
    ppermute x32, waiting for transfers between devices, swap(): return lax.ppermute(value, AXES, pairs)  52.6 us
    ppermute x32, starting transfers between devices, swap(): return lax.ppermute(value, AXES, pairs)  31.8 us
    pallas_call x2, Pallas kernels, backward(): pl.pallas_call(functools.partial(backward_kernel, s, heads), grid=(steps,...  28.8 us
    pallas_call x1, Pallas kernels, forward(): pl.pallas_call(functools.partial(forward_kernel, s, heads), grid=(rows //...  19.2 us
    pallas_call x1, Pallas kernels, finish(): pl.pallas_call(functools.partial(finish_kernel, s, far, chunks), grid_spe...  14.4 us
    unnamed x72, local copies, waits for them, and re-layouts  7.74 us
    pallas_call x2, Pallas kernels, combine(): pl.pallas_call(combine_kernel, grid=grid, in_specs=[spec, spec], out_spec...  7.17 us
  transfers between devices with their start and end apart: 32, of which 12 were waited for; matrix products, arithmetic and copies ran while one was open for 9% of the time, Pallas kernels for 33%

commit v1 on v0

--- a/solution.py
+++ b/solution.py
@@ -215,7 +215,7 @@
 
 
 def chosen_columns(s, keep_ref, tile, patches, wanted_hi):
-    row = keep_ref[pl.ds(tile, 1), :]
+    row = keep_ref[0, pl.ds(tile, 1), :]
     is_hi = tile < s.hi_each
     row = jnp.where(is_hi if wanted_hi else jnp.logical_not(is_hi), row, -1)
     column = jnp.broadcast_to(row.astype(F32), (LANES, LANES)).T.astype(jnp.int32)
@@ -252,7 +252,7 @@
     start = tn(picked, embed) + (nn(hot_hi, pos_hi_ref[...]) + nn(hot_lo, pos_lo_ref[...]))
     x0_ref[...] = start.astype(BF16)
     normed, _ = normalize(start)
-    normed = (normed * gain1_ref[...]).astype(BF16)
+    normed = (normed * gain1_ref[0:1, :]).astype(BF16)
     a_ref[...] = normed
     for c in range(3):
         part = slice(c * width, (c + 1) * width)
@@ -378,8 +378,8 @@
         for rows in subs:
             values = x1_ref[rows, :]
             normed, _ = normalize(values)
-            b_ref[rows, :] = (normed * gain2_ref[...]).astype(BF16)
-            forth_ref[rows, :] = values + b2_ref[...]
+            b_ref[rows, :] = (normed * gain2_ref[1:2, :]).astype(BF16)
+            forth_ref[rows, :] = values + b2_ref[2:3, :]
             back_ref[rows, :] = jnp.zeros((ROWS, width), F32)
             upward = tn(gpred_ref[:, rows], head).astype(BF16)
             gm_ref[rows, :] = upward
@@ -426,7 +426,7 @@
             normed, inverse = normalize(x1_ref[rows, :])
             part = jnp.sum(upward * normed, axis=0, keepdims=True)
             total = part if total is None else total + part
-            grad = gm_ref[rows, :].astype(F32) + normalize_back(upward, normed, inverse, gain2_ref[...])
+            grad = gm_ref[rows, :].astype(F32) + normalize_back(upward, normed, inverse, gain2_ref[1:2, :])
             grad = grad.astype(BF16)
             ga_ref[rows, :] = grad
             go_ref[rows, :] = nt(grad, wout_ref[...]).astype(BF16)
@@ -525,7 +525,7 @@
 def first_norm_back(gqkv, x0_ref, ga_ref, wqkv_ref, gain1_ref):
     upward = nt(gqkv, wqkv_ref[...])
     normed, inverse = normalize(x0_ref[...].astype(F32))
-    grad = ga_ref[...].astype(F32) + normalize_back(upward, normed, inverse, gain1_ref[...])
+    grad = ga_ref[...].astype(F32) + normalize_back(upward, normed, inverse, gain1_ref[0:1, :])
     return grad.astype(BF16), jnp.sum(upward * normed, axis=0, keepdims=True)
 
 
@@ -563,7 +563,7 @@
 def position_grads(s, keep_ref, g0, picked):
     hot_hi, hot_lo = [], []
     for t in range(s.tiles):
-        row = keep_ref[t : t + 1, :]
+        row = keep_ref[0, t : t + 1, :]
         patches = s.hi_patches if t < s.hi_each else s.lo_patches
         hot = jnp.where(iota((patches, LANES), 0) == row, 1.0, 0.0).astype(BF16)
         (hot_hi if t < s.hi_each else hot_lo).append(hot)
@@ -878,15 +878,16 @@
     member = lax.axis_index("var").astype(jnp.int32).reshape(1)
     s = Sizes(keep_lo.shape, keep_hi.shape, w_embed.shape, img_lo.shape, img_hi.shape, groups)
     features, width = s.features, s.width
-    gain1, gain2 = ln1_gain.reshape(1, -1), ln2_gain.reshape(1, -1)
+    gain1 = gain2 = vectors = jnp.stack([ln1_gain, ln2_gain, b_fc2])
     img_lo_t, img_hi_t = img_lo.transpose(0, 2, 1), img_hi.transpose(0, 2, 1)
 
     own = jnp.concatenate([w_embed, w_head.T], axis=0)
     crossed = swap(own, 0, 2)
-    weights = [own, swap(own, 0, 1), crossed, swap(crossed, 0, 1)]
-    sent = pick(s, (1, 2, 3), member, keep_lo, keep_hi, img_lo_t, img_hi_t)
-    picked = [swap(value, 0, k + 1) for k, value in enumerate(sent)]
-    picked = [*pick(s, (0,), member, keep_lo, keep_hi, img_lo_t, img_hi_t), *picked]
+    beside = swap(own, 0, 1)
+    sent = pick(s, (2, 3, 1, 0), member, keep_lo, keep_hi, img_lo_t, img_hi_t)
+    crossed = tie(crossed, sent[0])
+    weights = [own, beside, crossed, swap(crossed, 0, 1)]
+    picked = [sent[3], swap(sent[2], 0, 1), swap(sent[0], 0, 2), swap(sent[1], 0, 3)]
     keep, seen, *cots = stage(
         s,
         tie(member, sent[0]),
@@ -898,7 +899,7 @@
         cot_hi.transpose(0, 2, 1),
     )
     cots = exchange_relative(cots)
-    own_keep = keep[0]
+    own_keep = keep
     x0, a, qkv, probs, mixed, x1 = forward(
         s, HEADS, own_keep, seen, picked, weights, pos_lo, pos_hi, gain1, w_qkv, w_out
     )
@@ -947,7 +948,7 @@
         w_fc1,
         b_fc1.reshape(1, -1),
         w_fc2,
-        b_fc2.reshape(1, -1),
+        vectors,
         gain2,
         w_out,
     )
@@ -965,12 +966,16 @@
     if cube:
         for chain in (two, one, out, head):
             chain.hold(parts[0][0])
-    near_tokens = [step("x", two, out, head), step("y", one)]
+    near_tokens = [step("x", two), step("y", one)]
+    if cube:
+        for chain in (out, head):
+            chain.hold(two.held, one.held)
+    near_tokens.append(step("z0", out, head))
     parts.append(back(1, s.rows // ROWS - 1, parts[0][0], two.held, one.held, *tokens))
     if cube:
         for chain in (two, one, out, head):
             chain.hold(parts[1][0])
-    tokens = [step("y", two, out, head), step("x", one)]
+    tokens = [step("y", two), step("x", one, out, head)]
     gqkvs, g0s, gains = zip(*parts)
     near, sent, near_embed, sent_embed, *blocks = finish(
         s,
@@ -993,22 +998,24 @@
         for chain in old:
             chain.hold(first.got)
         one_half, other_half = halves_of(first)
-        tokens = [trade("x", one_half, embed), trade("y", other_half)]
-        trade("z0", *old)
+        tokens = [trade("x", one_half, embed), trade("y", other_half, out, head)]
+        trade("z0", two, one)
         for chain in old:
             chain.hold(*tokens)
         tokens = [trade("y", one_half, embed), trade("x", other_half)]
         trade("z1", *old)
         blocks = [tie(block_of, *tokens) for block_of in blocks]
         trade("z0", one_half, other_half, embed)
-        token = trade("z1", one_half, other_half, embed)
-        for chain in old:
-            chain.hold(token)
-        last_member = tie(member, token)
-        grad_fc2, grad_fc1, rest, grad_head, grad_embed = (
-            chain.final() for chain in (two, one, out, head, embed)
+        trade("z1", one_half, other_half, embed)
+        head.hold(embed.held)
+        grad_head = both_halves(head.final())
+        last_member = tie(member, grad_head)
+        for chain in (two, one, out):
+            chain.hold(grad_head)
+        grad_fc2, grad_fc1, rest, grad_embed = (
+            chain.final() for chain in (two, one, out, embed)
         )
-        grad_head, grad_embed = both_halves(grad_head), both_halves(grad_embed)
+        grad_embed = both_halves(grad_embed)
         first = jnp.concatenate([one_half.final(), other_half.final()], axis=0).reshape(-1, width)
         grad_fc1 = grad_fc1.reshape(-1, width)
     else:

time: 259 us -> 254 us (0.981)
  waiting for transfers between devices: 52.6 us -> 47.6 us
  starting transfers between devices: 31.8 us -> 34.6 us
    ppermute x32 -> x33, waiting for transfers between devices: 52.6 us -> 47.6 us  [swap(): return lax.ppermute(value, AXES, pairs)]
    ppermute x32 -> x33, starting transfers between devices: 31.8 us -> 34.6 us  [swap(): return lax.ppermute(value, AXES, pairs)]
    pallas_call x2 -> x1, Pallas kernels: 6.21 us -> 3.65 us  [pick(): pl.pallas_call(functools.partial(pick_kernel, s, members), grid_spec=pltp...]
    unnamed x72 -> x66, local copies, waits for them, and re-layouts: 7.74 us -> 6.89 us
  transfers between devices with their start and end apart: 32 -> 33, of which waited for: 12 -> 15; matrix products, arithmetic and copies ran while one was open for 9% -> 9% of each run, Pallas kernels for 33% -> 27%
where the time goes in v1:
time: 254 us; the launch traced here: 249 us
  Pallas kernels  137 us (54%)
  waiting for transfers between devices  47.6 us (19%)
  starting transfers between devices  34.6 us (14%)
  local copies, waits for them, and re-layouts  16.7 us (7%)
  other arithmetic  11.9 us (5%)
    pallas_call x1, Pallas kernels, hidden(): pl.pallas_call(functools.partial(hidden_kernel, s, far, chunks), grid_spe...  55.4 us
    ppermute x33, waiting for transfers between devices, swap(): return lax.ppermute(value, AXES, pairs)  47.6 us
    ppermute x33, starting transfers between devices, swap(): return lax.ppermute(value, AXES, pairs)  34.6 us
    pallas_call x2, Pallas kernels, backward(): pl.pallas_call(functools.partial(backward_kernel, s, heads), grid=(steps,...  28.7 us
    pallas_call x1, Pallas kernels, forward(): pl.pallas_call(functools.partial(forward_kernel, s, heads), grid=(rows //...  19.2 us
    pallas_call x1, Pallas kernels, finish(): pl.pallas_call(functools.partial(finish_kernel, s, far, chunks), grid_spe...  14.3 us
    pallas_call x2, Pallas kernels, combine(): pl.pallas_call(combine_kernel, grid=grid, in_specs=[spec, spec], out_spec...  8.38 us
    unnamed x66, local copies, waits for them, and re-layouts  6.89 us
  transfers between devices with their start and end apart: 33, of which 15 were waited for; matrix products, arithmetic and copies ran while one was open for 9% of the time, Pallas kernels for 27%

profile of v1, /device:TPU:0, one launch (start us, length us, event | category | flops | bytes accessed | tf_op | source)
XLA Modules:
  0.0 248.9 jit_solution(3732091030959211171)
XLA Ops:
  1.6 3.0 %collective-permute-start.4 = (bf16[160,768]{1,0:T(8,128)(2,1)S(1)}, bf16[160,768]{1,0:T(8,128)(2,1)S(1)}, u32[]{:S(2)}, u32[]{:S(2)}) collective-permute-start(bf16[160,768]{1,0:T(8,128)(2,1)S(1)} %pad_maximum_fusion.8.w0.h0), channel_id=1, source_target_pairs={{0,2},{1,3},{2,0},{3,1},{4,6},{5,7},{6,4},{7,5},{8,10},{9,11},{10,... | collective-permute-start | bytes 737288 | tf_op jit(solution)/shard_map/ppermute | solution.py:738
  6.1 3.6 %shard_map.315 = (bf16[80,1024]{1,0:T(8,128)(2,1)}, bf16[80,1024]{1,0:T(8,128)(2,1)}, bf16[80,1024]{1,0:T(8,128)(2,1)}, bf16[80,1024]{1,0:T(8,128)(2,1)}) custom-call(s32[1]{0:T(128)} %bitcast.member_ref, s32[40,32]{1,0:T(8,128)} %copy.88.keep_lo_ref, s32[20,128]{1,0:T(8,128)} %keep_hi_ref.3, bf16[40,80,128]{2,1,0:T(8,128)(2,1)} %bitcast.251, ...), custom_call_target="tpu_custom_call" | custom-call | flops 1000000000 | bytes 2000000 | tf_op jit(solution)/shard_map/pallas_call | solution.py:158
  14.1 2.3 shard_map.316
  17.8 1.8 collective-permute-start.7
  22.9 19.2 %shard_map.317 = (bf16[1024,768]{1,0:T(8,128)(2,1)}, bf16[1024,768]{1,0:T(8,128)(2,1)}, bf16[1024,2304]{1,0:T(8,128)(2,1)}, bf16[8,6,256,128]{3,2,1,0:T(8,128)(2...) custom-call(s32[4,8,128]{2,1,0:T(8,128)} %get-tuple-element.128.keep_ref, f32[8,128]{1,0:T(8,128)} %get-tuple-element.134.seen_ref, ...), custom_call_target="tpu_custom_call" | custom-call | flops 7500000256 | bytes 15000000 | tf_op jit(solution)/shard_map/pallas_call | solution.py:285
  42.9 55.4 %shard_map.318 = (bf16[2,2,4,96,768]{4,3,2,1,0:T(8,128)(2,1)}, bf16[2,2,4,96,768]{4,3,2,1,0:T(8,128)(2,1)}, bf16[4,384,768]{2,1,0:T(8,128)(2,1)}, bf16[4,384,768...) custom-call(s32[2]{0:T(128)} %pad_add_fusion.ids_ref, ...), custom_call_target="tpu_custom_call" | custom-call | flops 16999999488 | bytes 20000000 | tf_op jit(solution)/shard_map/pallas_call | solution.py:469
  99.3 8.7 %shard_map.319 = (bf16[256,2304]{1,0:T(8,128)(2,1)}, bf16[256,768]{1,0:T(8,128)(2,1)}, f32[1,768]{1,0:T(1,128)}) custom-call(bf16[1024,2304]{1,0:T(8,128)(2,1)} %get-tuple-element.142.qkv_ref, bf16[8,6,256,128]{3,2,1,0:T(8,128)(2,1)} %get-tuple-element.143.probs_ref, bf16[1024,768]{1,0:T(8,128)(2,1)} %get-tuple-element.144.go_ref, ...), custom_call_target="tpu_custom_call" | custom-call | flops 4000000000 | bytes 3000000 | tf_op jit(solution)/shard_map/pallas_call | solution.py:552
  108.1 4.7 %shard_map.321 = (bf16[8,96,768]{2,1,0:T(8,128)(2,1)}, bf16[8,96,768]{2,1,0:T(8,128)(2,1)}) custom-call(bf16[8,2,96,768]{3,2,1,0:T(8,128)(2,1)} %bitcast.194, bf16[8,2,96,768]{3,2,1,0:T(8,128)(2,1)} %bitcast.20.got_ref), custom_call_target="tpu_custom_call" | custom-call | flops 500000 | bytes 1769472 | tf_op jit(solution)/shard_map/pallas_call | solution.py:672
  112.9 3.7 %shard_map.320 = (bf16[1,768,768]{2,1,0:T(8,128)(2,1)}, bf16[1,768,768]{2,1,0:T(8,128)(2,1)}) custom-call(bf16[1,2,768,768]{3,2,1,0:T(8,128)(2,1)} %bitcast.193, bf16[1,2,768,768]{3,2,1,0:T(8,128)(2,1)} %bitcast.195), custom_call_target="tpu_custom_call" | custom-call | flops 500000 | bytes 1769472 | tf_op jit(solution)/shard_map/pallas_call | solution.py:672
  122.2 20.0 %shard_map.322 = (bf16[768,2304]{1,0:T(8,128)(2,1)}, bf16[768,768]{1,0:T(8,128)(2,1)}, f32[1,768]{1,0:T(1,128)}) custom-call(bf16[1024,2304]{1,0:T(8,128)(2,1)} %get-tuple-element.142.qkv_ref, bf16[8,6,256,128]{3,2,1,0:T(8,128)(2,1)} %get-tuple-element.143.probs_ref, bf16[1024,768]{1,0:T(8,128)(2,1)} %get-tuple-element.144.go_ref, ...), custom_call_target="tpu_custom_call" | custom-call | flops 12000000000 | bytes 9000000 | tf_op jit(solution)/shard_map/pallas_call | solution.py:552
  146.2 2.0 collective-permute-done.14
  152.8 14.3 %shard_map.323 = (bf16[4,384,768]{2,1,0:T(8,128)(2,1)}, bf16[4,384,768]{2,1,0:T(8,128)(2,1)}, bf16[2,2,40,768]{3,2,1,0:T(8,128)(2,1)}, bf16[2,2,40,768]{3,2,1,0:...) custom-call(s32[2]{0:T(128)} %pad_add_fusion.ids_ref, ...), custom_call_target="tpu_custom_call" | custom-call | flops 3500000000 | bytes 6000000 | tf_op jit(solution)/shard_map/pallas_call | solution.py:628
  167.2 3.9 %collective-permute-done.15 = bf16[592,768]{1,0:T(8,128)(2,1)S(1)} collective-permute-done((bf16[592,768]{1,0:T(8,128)(2,1)}, bf16[592,768]{1,0:T(8,128)(2,1)S(1)}, u32[]{:S(2)}, u32[]{:S(2)}) %collective-permute-start.15) | collective-permute-done | bytes 909344 | tf_op jit(solution)/shard_map/ppermute | solution.py:738
  173.4 2.1 collective-permute-done.20
  181.1 11.4 %collective-permute-done.22 = bf16[384,768]{1,0:T(8,128)(2,1)S(1)} collective-permute-done((bf16[384,768]{1,0:T(8,128)(2,1)S(1)}, bf16[384,768]{1,0:T(8,128)(2,1)S(1)}, u32[]{:S(2)}, u32[]{:S(2)}) %collective-permute-start.22) | collective-permute-done | bytes 589856 | tf_op jit(solution)/shard_map/ppermute | solution.py:738
  192.5 3.1 %collective-permute-done.21 = bf16[464,768]{1,0:T(8,128)(2,1)S(1)} collective-permute-done((bf16[464,768]{1,0:T(8,128)(2,1)S(1)}, bf16[464,768]{1,0:T(8,128)(2,1)S(1)}, u32[]{:S(2)}, u32[]{:S(2)}) %collective-permute-start.21) | collective-permute-done | bytes 712736 | tf_op jit(solution)/shard_map/ppermute | solution.py:738
  198.8 2.3 collective-permute-start.25
  201.4 2.8 %collective-permute-start.23 = (bf16[264,768]{1,0:T(8,128)(2,1)S(1)}, bf16[264,768]{1,0:T(8,128)(2,1)S(1)}, u32[]{:S(2)}, u32[]{:S(2)}) collective-permute-start(bf16[264,768]{1,0:T(8,128)(2,1)S(1)} %pad_maximum_fusion.5), channel_id=1, source_target_pairs={{0,16},{1,17},{2,18},{3,19},{4,20},{5,21},{6,22},{7,23},{8,24},{9,... | collective-permute-start | bytes 1216520 | tf_op jit(solution)/shard_map/ppermute | solution.py:738
  204.2 2.5 collective-permute-done.25
  210.5 9.7 %collective-permute-done.23 = bf16[264,768]{1,0:T(8,128)(2,1)S(1)} collective-permute-done((bf16[264,768]{1,0:T(8,128)(2,1)S(1)}, bf16[264,768]{1,0:T(8,128)(2,1)S(1)}, u32[]{:S(2)}, u32[]{:S(2)}) %collective-permute-start.23) | collective-permute-done | bytes 405536 | tf_op jit(solution)/shard_map/ppermute | solution.py:738
  220.3 2.2 collective-permute-done.26
  222.6 2.7 %collective-permute-start.31 = (bf16[136,768]{1,0:T(8,128)(2,1)S(1)}, bf16[136,768]{1,0:T(8,128)(2,1)S(1)}, u32[]{:S(2)}, u32[]{:S(2)}) collective-permute-start(bf16[136,768]{1,0:T(8,128)(2,1)S(1)} %pad_maximum_fusion.10), channel_id=1, source_target_pairs={{0,16},{1,17},{2,18},{3,19},{4,20},{5,21},{6,22},{7,23},{8,24},{9,... | collective-permute-start | bytes 626696 | tf_op jit(solution)/shard_map/ppermute | solution.py:738
  226.9 6.0 %collective-permute-done.31 = bf16[136,768]{1,0:T(8,128)(2,1)S(1)} collective-permute-done((bf16[136,768]{1,0:T(8,128)(2,1)S(1)}, bf16[136,768]{1,0:T(8,128)(2,1)S(1)}, u32[]{:S(2)}, u32[]{:S(2)}) %collective-permute-start.31) | collective-permute-done | bytes 208928 | tf_op jit(solution)/shard_map/ppermute | solution.py:738
  244.1 4.6 %shard_map.324 = (bf16[40,80,128]{2,1,0:T(8,128)(2,1)}, bf16[20,80,512]{2,1,0:T(8,128)(2,1)}, bf16[1280,80]{1,0:T(8,128)(2,1)}, bf16[20,80,128]{2,1,0:T(8,128)(2,1)}) custom-call(s32[1]{0:T(128)} %bitcast.member_ref, s32[4,8,128]{2,1,0:T(8,128)} %get-tuple-element.128.keep_ref, bf16[160,1024]{1,0:T(8,128)(2,1)} %get-tuple-element.217.r0, ...), custom_call_target="tpu_custom_call" | custom-call | flops 1000000000 | bytes 4000000 | tf_op jit(solution)/shard_map/pallas_call | solution.py:719
  (217 shorter events, 55.2 us)
Async XLA Ops:
  4.6 17.5 %collective-permute-start.3 = (bf16[160,768]{1,0:T(8,128)(2,1)S(1)}, bf16[160,768]{1,0:T(8,128)(2,1)S(1)}, u32[]{:S(2)}, u32[]{:S(2)}) collective-permute-start(bf16[160,768]{1,0:T(8,128)(2,1)S(1)} %pad_maximum_fusion.8.w0.h0), channel_id=1, source_target_pairs={{0,1},{1,0},{2,3},{3,2},{4,5},{5,4},{6,7},{7,6},{8,9},{9,8},{10,11... | collective-permute-start | bytes 737288 | tf_op jit(solution)/shard_map/ppermute | solution.py:738
  10.6 11.5 %collective-permute-start.5 = (bf16[160,768]{1,0:T(8,128)(2,1)S(1)}, bf16[160,768]{1,0:T(8,128)(2,1)S(1)}, u32[]{:S(2)}, u32[]{:S(2)}) collective-permute-start(bf16[160,768]{1,0:T(8,128)(2,1)S(1)} %collective-permute-done.4.w2.h2), channel_id=1, source_target_pairs={{0,1},{1,0},{2,3},{3,2},{4,5},{5,4},{6,7},{7,6},{8,9},{9,8},{10,11... | collective-permute-start | bytes 737288 | tf_op jit(solution)/shard_map/ppermute | solution.py:738
  17.8 24.2 %collective-permute-start.6 = (bf16[80,1024]{1,0:T(8,128)(2,1)}, bf16[80,1024]{1,0:T(8,128)(2,1)S(1)}, u32[]{:S(2)}, u32[]{:S(2)}) collective-permute-start(bf16[80,1024]{1,0:T(8,128)(2,1)} %get-tuple-element.136), channel_id=1, source_target_pairs={{0,1},{1,0},{2,3},{3,2},{4,5},{5,4},{6,7},{7,6},{8,9},{9,8},{10,11... | collective-permute-start | bytes 491528 | tf_op jit(solution)/shard_map/ppermute | solution.py:738
  17.8 24.2 %collective-permute-start.7 = (bf16[80,1024]{1,0:T(8,128)(2,1)}, bf16[80,1024]{1,0:T(8,128)(2,1)S(1)}, u32[]{:S(2)}, u32[]{:S(2)}) collective-permute-start(bf16[80,1024]{1,0:T(8,128)(2,1)} %get-tuple-element.137), channel_id=1, source_target_pairs={{0,2},{1,3},{2,0},{3,1},{4,6},{5,7},{6,4},{7,5},{8,10},{9,11},{10,... | collective-permute-start | bytes 491528 | tf_op jit(solution)/shard_map/ppermute | solution.py:738
  20.6 21.5 %collective-permute-start.8 = (bf16[80,1024]{1,0:T(8,128)(2,1)}, bf16[80,1024]{1,0:T(8,128)(2,1)S(1)}, u32[]{:S(2)}, u32[]{:S(2)}) collective-permute-start(bf16[80,1024]{1,0:T(8,128)(2,1)} %get-tuple-element.138), channel_id=1, source_target_pairs={{0,3},{1,2},{2,1},{3,0},{4,7},{5,6},{6,5},{7,4},{8,11},{9,10},{10,... | collective-permute-start | bytes 491528 | tf_op jit(solution)/shard_map/ppermute | solution.py:738
  98.2 9.8 %collective-permute-start.11 = (bf16[1536,768]{1,0:T(8,128)(2,1)}, bf16[1536,768]{1,0:T(8,128)(2,1)}, u32[]{:S(2)}, u32[]{:S(2)}) collective-permute-start(bf16[1536,768]{1,0:T(8,128)(2,1)} %bitcast.249), channel_id=1, source_target_pairs={{0,1},{1,0},{2,3},{3,2},{4,5},{5,4},{6,7},{7,6},{8,9},{9,8},{10,11... | collective-permute-start | bytes 7077896 | tf_op jit(solution)/shard_map/ppermute | solution.py:738
  98.6 9.5 %collective-permute-start.10 = (bf16[1536,768]{1,0:T(8,128)(2,1)}, bf16[1536,768]{1,0:T(8,128)(2,1)S(1)}, u32[]{:S(2)}, u32[]{:S(2)}) collective-permute-start(bf16[1536,768]{1,0:T(8,128)(2,1)} %bitcast.248), channel_id=1, source_target_pairs={{0,1},{1,0},{2,3},{3,2},{4,5},{5,4},{6,7},{7,6},{8,9},{9,8},{10,11... | collective-permute-start | bytes 7077896 | tf_op jit(solution)/shard_map/ppermute | solution.py:738
  98.8 9.2 %collective-permute-start.12 = (bf16[512,768]{1,0:T(8,128)(2,1)}, bf16[512,768]{1,0:T(8,128)(2,1)S(1)}, u32[]{:S(2)}, u32[]{:S(2)}) collective-permute-start(bf16[512,768]{1,0:T(8,128)(2,1)} %bitcast.252), channel_id=1, source_target_pairs={{0,1},{1,0},{2,3},{3,2},{4,5},{5,4},{6,7},{7,6},{8,9},{9,8},{10,11... | collective-permute-start | bytes 2359304 | tf_op jit(solution)/shard_map/ppermute | solution.py:738
  118.5 24.8 %collective-permute-start.13 = (bf16[416,768]{1,0:T(8,128)(2,1)}, bf16[416,768]{1,0:T(8,128)(2,1)}, u32[]{:S(2)}, u32[]{:S(2)}) collective-permute-start(bf16[416,768]{1,0:T(8,128)(2,1)} %pad_maximum_fusion.3), channel_id=1, source_target_pairs={{0,8},{1,9},{2,10},{3,11},{4,12},{5,13},{6,14},{7,15},{8,0},{9,1},... | collective-permute-start | bytes 1916936 | tf_op jit(solution)/shard_map/ppermute | solution.py:738
  120.1 28.1 %collective-permute-start.14 = (bf16[768,768]{1,0:T(8,128)(2,1)}, bf16[768,768]{1,0:T(8,128)(2,1)S(1)}, u32[]{:S(2)}, u32[]{:S(2)}) collective-permute-start(bf16[768,768]{1,0:T(8,128)(2,1)} %bitcast.29), channel_id=1, source_target_pairs={{0,4},{1,5},{2,6},{3,7},{4,0},{5,1},{6,2},{7,3},{8,12},{9,13},{10,... | collective-permute-start | bytes 3538952 | tf_op jit(solution)/shard_map/ppermute | solution.py:738
  121.7 28.4 %collective-permute-start.16 = (bf16[768,768]{1,0:T(8,128)(2,1)}, bf16[768,768]{1,0:T(8,128)(2,1)S(1)}, u32[]{:S(2)}, u32[]{:S(2)}) collective-permute-start(bf16[768,768]{1,0:T(8,128)(2,1)} %bitcast.37), channel_id=1, source_target_pairs={{0,2},{1,3},{2,0},{3,1},{4,6},{5,7},{6,4},{7,5},{8,10},{9,11},{10,... | collective-permute-start | bytes 3538952 | tf_op jit(solution)/shard_map/ppermute | solution.py:738
  149.6 21.5 %collective-permute-start.15 = (bf16[592,768]{1,0:T(8,128)(2,1)}, bf16[592,768]{1,0:T(8,128)(2,1)S(1)}, u32[]{:S(2)}, u32[]{:S(2)}) collective-permute-start(bf16[592,768]{1,0:T(8,128)(2,1)} %pad_maximum_fusion), channel_id=1, source_target_pairs={{0,2},{1,3},{2,0},{3,1},{4,6},{5,7},{6,4},{7,5},{8,10},{9,11},{10,... | collective-permute-start | bytes 2727944 | tf_op jit(solution)/shard_map/ppermute | solution.py:738
  151.1 19.9 %collective-permute-start.17 = (bf16[384,768]{1,0:T(8,128)(2,1)}, bf16[384,768]{1,0:T(8,128)(2,1)S(1)}, u32[]{:S(2)}, u32[]{:S(2)}) collective-permute-start(bf16[384,768]{1,0:T(8,128)(2,1)} %bitcast.41), channel_id=1, source_target_pairs={{0,4},{1,5},{2,6},{3,7},{4,0},{5,1},{6,2},{7,3},{8,12},{9,13},{10,... | collective-permute-start | bytes 1769480 | tf_op jit(solution)/shard_map/ppermute | solution.py:738
  176.8 15.7 %collective-permute-start.22 = (bf16[384,768]{1,0:T(8,128)(2,1)S(1)}, bf16[384,768]{1,0:T(8,128)(2,1)S(1)}, u32[]{:S(2)}, u32[]{:S(2)}) collective-permute-start(bf16[384,768]{1,0:T(8,128)(2,1)S(1)} %pad_maximum_fusion.4), channel_id=1, source_target_pairs={{0,8},{1,9},{2,10},{3,11},{4,12},{5,13},{6,14},{7,15},{8,0},{9,1},... | collective-permute-start | bytes 1769480 | tf_op jit(solution)/shard_map/ppermute | solution.py:738
  177.6 18.0 %collective-permute-start.21 = (bf16[464,768]{1,0:T(8,128)(2,1)S(1)}, bf16[464,768]{1,0:T(8,128)(2,1)S(1)}, u32[]{:S(2)}, u32[]{:S(2)}) collective-permute-start(bf16[464,768]{1,0:T(8,128)(2,1)S(1)} %pad_maximum_fusion.2), channel_id=1, source_target_pairs={{0,2},{1,3},{2,0},{3,1},{4,6},{5,7},{6,4},{7,5},{8,10},{9,11},{10,... | collective-permute-start | bytes 2138120 | tf_op jit(solution)/shard_map/ppermute | solution.py:738
  179.4 18.5 %collective-permute-start.19 = (bf16[488,768]{1,0:T(8,128)(2,1)S(1)}, bf16[488,768]{1,0:T(8,128)(2,1)S(1)}, u32[]{:S(2)}, u32[]{:S(2)}) collective-permute-start(bf16[488,768]{1,0:T(8,128)(2,1)S(1)} %pad_maximum_fusion.1), channel_id=1, source_target_pairs={{0,4},{1,5},{2,6},{3,7},{4,0},{5,1},{6,2},{7,3},{8,12},{9,13},{10,... | collective-permute-start | bytes 2248712 | tf_op jit(solution)/shard_map/ppermute | solution.py:738
  196.0 10.7 %collective-permute-start.24 = (bf16[232,768]{1,0:T(8,128)(2,1)S(1)}, bf16[232,768]{1,0:T(8,128)(2,1)S(1)}, u32[]{:S(2)}, u32[]{:S(2)}) collective-permute-start(bf16[232,768]{1,0:T(8,128)(2,1)S(1)} %pad_maximum_fusion.6), channel_id=1, source_target_pairs={{0,4},{1,5},{2,6},{3,7},{4,0},{5,1},{6,2},{7,3},{8,12},{9,13},{10,... | collective-permute-start | bytes 1069064 | tf_op jit(solution)/shard_map/ppermute | solution.py:738
  201.4 18.8 %collective-permute-start.23 = (bf16[264,768]{1,0:T(8,128)(2,1)S(1)}, bf16[264,768]{1,0:T(8,128)(2,1)S(1)}, u32[]{:S(2)}, u32[]{:S(2)}) collective-permute-start(bf16[264,768]{1,0:T(8,128)(2,1)S(1)} %pad_maximum_fusion.5), channel_id=1, source_target_pairs={{0,16},{1,17},{2,18},{3,19},{4,20},{5,21},{6,22},{7,23},{8,24},{9,... | collective-permute-start | bytes 1216520 | tf_op jit(solution)/shard_map/ppermute | solution.py:738
  207.0 15.5 %collective-permute-start.26 = (bf16[232,768]{1,0:T(8,128)(2,1)S(1)}, bf16[232,768]{1,0:T(8,128)(2,1)S(1)}, u32[]{:S(2)}, u32[]{:S(2)}) collective-permute-start(bf16[232,768]{1,0:T(8,128)(2,1)S(1)} %pad_maximum_fusion.7), channel_id=1, source_target_pairs={{0,8},{1,9},{2,10},{3,11},{4,12},{5,13},{6,14},{7,15},{8,0},{9,1},... | collective-permute-start | bytes 1069064 | tf_op jit(solution)/shard_map/ppermute | solution.py:738
  208.6 35.5 %collective-permute-start.30 = (bf16[160,1024]{1,0:T(8,128)(2,1)S(1)}, bf16[160,1024]{1,0:T(8,128)(2,1)}, u32[]{:S(2)}, u32[]{:S(2)}) collective-permute-start(bf16[160,1024]{1,0:T(8,128)(2,1)S(1)} %copy-done.20), channel_id=1, source_target_pairs={{0,3},{1,2},{2,1},{3,0},{4,7},{5,6},{6,5},{7,4},{8,11},{9,10},{10,... | collective-permute-start | bytes 983048 | tf_op jit(solution)/shard_map/ppermute | solution.py:738
  208.6 35.5 %collective-permute-start.29 = (bf16[160,1024]{1,0:T(8,128)(2,1)S(1)}, bf16[160,1024]{1,0:T(8,128)(2,1)}, u32[]{:S(2)}, u32[]{:S(2)}) collective-permute-start(bf16[160,1024]{1,0:T(8,128)(2,1)S(1)} %copy-done.19), channel_id=1, source_target_pairs={{0,2},{1,3},{2,0},{3,1},{4,6},{5,7},{6,4},{7,5},{8,10},{9,11},{10,... | collective-permute-start | bytes 983048 | tf_op jit(solution)/shard_map/ppermute | solution.py:738
  210.3 33.8 %collective-permute-start.28 = (bf16[160,1024]{1,0:T(8,128)(2,1)S(1)}, bf16[160,1024]{1,0:T(8,128)(2,1)}, u32[]{:S(2)}, u32[]{:S(2)}) collective-permute-start(bf16[160,1024]{1,0:T(8,128)(2,1)S(1)} %copy-done.18), channel_id=1, source_target_pairs={{0,1},{1,0},{2,3},{3,2},{4,5},{5,4},{6,7},{7,6},{8,9},{9,8},{10,11... | collective-permute-start | bytes 983048 | tf_op jit(solution)/shard_map/ppermute | solution.py:738
  222.6 10.3 %collective-permute-start.31 = (bf16[136,768]{1,0:T(8,128)(2,1)S(1)}, bf16[136,768]{1,0:T(8,128)(2,1)S(1)}, u32[]{:S(2)}, u32[]{:S(2)}) collective-permute-start(bf16[136,768]{1,0:T(8,128)(2,1)S(1)} %pad_maximum_fusion.10), channel_id=1, source_target_pairs={{0,16},{1,17},{2,18},{3,19},{4,20},{5,21},{6,22},{7,23},{8,24},{9,... | collective-permute-start | bytes 626696 | tf_op jit(solution)/shard_map/ppermute | solution.py:738
  225.3 12.0 %collective-permute-start.27 = (bf16[40,768]{1,0:T(8,128)(2,1)S(1)}, bf16[40,768]{1,0:T(8,128)(2,1)S(1)}, u32[]{:S(2)}, u32[]{:S(2)}) collective-permute-start(bf16[40,768]{1,0:T(8,128)(2,1)S(1)} %add_convert_fusion.38), channel_id=1, source_target_pairs={{0,4},{1,5},{2,6},{3,7},{4,0},{5,1},{6,2},{7,3},{8,12},{9,13},{10,... | collective-permute-start | bytes 184328 | tf_op jit(solution)/shard_map/ppermute | solution.py:738
  (46 other events, 187.1 us)
